TPU v7x, 512 devices: a whole 4x4x16 slice. The times are simulated.
512 devices in a mesh: swath: 32 (over z, core), chan: 16 (over x, y).
Axes of the slice: x: 4, y: 4, z: 16, core: 2. Of those that a mesh axis runs over, the one named last changes fastest.
Arguments:
- grid_profiles: bfloat16 [32768, 256], P('swath'), may hold values from -6 to 6
- send_lists: int32 [32, 32, 128], P('swath'), may hold values from 0 to 1023
- counts: int32 [32, 32], P('swath'), may hold values from 1 to 128, as said below
- angle_index: int32 [128], replicated, may hold values from 0 to 7
- jacobian: bfloat16 [3, 256, 608], P(None, None, 'chan'), may hold values from -0.375 to 0.375
- observed: bfloat16 [608, 131072], P('chan', 'swath'), may hold values from -6 to 6
- kappa: float32 [2, 608], P(None, 'chan'), may hold values from 0.04 to 0.24
- factor: bfloat16 [608, 608], P('chan')
Outputs:
- weighted: float32 [608, 131072], P('chan', 'swath')
Inputs may be any that keep to these rules, and one draw needn't show every extreme that they name: `counts`: some receiver gets 128 live slots from every sender; every entry is at least one.
All inputs are finite; a program needn't handle non-finite values.
Results may differ from a plain program's by a relative error of at most 0.0029.
Values may be sent and summed in bfloat16 or wider, within the bound.
A program may use at most 64 MiB of HBM per device.

v0:
```python
import math

import jax
import jax.numpy as jnp
from jax import lax
from jax.sharding import PartitionSpec as P

XTRACK = 128
NANG = 8


max_zenith = math.pi / 3.0


def extended_2(block, sides, width):
    for axis, dim in sides:
        count = lax.axis_size(axis)
        forward = [(i, i + 1) for i in range(count - 1)]
        backward = [(target, source) for source, target in forward]
        low = lax.ppermute(
            lax.slice_in_dim(block, block.shape[dim] - width, None, axis=dim), axis, forward
        )
        high = lax.ppermute(lax.slice_in_dim(block, 0, width, axis=dim), axis, backward)
        block = jnp.concatenate([low, block, high], axis=dim)
    return block


def diffuse_once(extended, along_rate, cross_rate):
    center = extended[:, 1:-1]
    along_sum = extended[:, 2:] + extended[:, :-2] - 2.0 * center
    side_pad = jnp.pad(center, ((0, 0), (0, 0), (1, 1)))
    cross_sum = side_pad[:, :, 2:] + side_pad[:, :, :-2] - 2.0 * center
    return center + along_rate * along_sum + cross_rate * cross_sum


def line_rims(smooth_field):
    return extended_2(smooth_field, (("swath", 1),), 1)


def on_device(grid_profiles, send_lists, counts, angle_index, jacobian, observed, kappa, factor):
    slot_rows = send_lists[0]
    slots = slot_rows.shape[1]
    own_chan = observed.shape[0]
    pixel_count = observed.shape[1]
    line_count = pixel_count // XTRACK
    live_slot = jnp.arange(slots, dtype=jnp.int32)[None, :] < counts[0][:, None]
    zero_value = jnp.zeros((), grid_profiles.dtype)
    outgoing = jnp.where(live_slot[:, :, None], grid_profiles[slot_rows], zero_value)
    incoming = lax.all_to_all(outgoing, "swath", split_axis=0, concat_axis=0, tiled=True)
    pixel_profiles = incoming.reshape(pixel_count, grid_profiles.shape[1])
    model = jnp.einsum("mkc,pk->mcp", jacobian, pixel_profiles, preferred_element_type=jnp.float32)
    zenith = angle_index.astype(jnp.float32) * (max_zenith / (NANG - 1))
    slant_path = 1.0 / jnp.cos(zenith) - 1.0
    model = model.reshape(3, own_chan, line_count, XTRACK)
    departure = observed.astype(jnp.float32).reshape(own_chan, line_count, XTRACK) - (
        model[0] + slant_path * model[1] + slant_path * slant_path * model[2]
    )
    along_rate = kappa[0][:, None, None]
    cross_rate = kappa[1][:, None, None]
    smooth_field = departure
    for sweep in range(3):
        smooth_field = diffuse_once(line_rims(smooth_field), along_rate, cross_rate)
    smoothed = smooth_field.reshape(own_chan, pixel_count).astype(jnp.bfloat16)
    return jnp.dot(
        factor,
        lax.all_gather(smoothed, "chan", axis=0, tiled=True),
        preferred_element_type=jnp.float32,
    )


def solution(mesh):
    in_specs = (
        P("swath", None),
        P("swath", None, None),
        P("swath", None),
        P(),
        P(None, None, "chan"),
        P("chan", "swath"),
        P(None, "chan"),
        P("chan", None),
    )
    out_specs = P("chan", "swath")
    return jax.shard_map(
        on_device, mesh=mesh, in_specs=in_specs, out_specs=out_specs, check_vma=False
    )
```

profile of v0, /device:TPU:1, one launch (start us, length us, event | category | flops | bytes accessed | tf_op | source)
XLA Modules:
  0.0 252.0 jit_solution(1715933017502331585)
XLA Ops:
  6.5 0.0 copy-start
  6.5 0.8 iota_compare_fusion
  7.3 0.7 fusion.29
  8.0 0.0 copy-done
  8.1 14.6 %gather_fusion = bf16[4096,256]{1,0:T(8,128)(2,1)S(1)} fusion(bf16[1024,256]{1,0:T(8,128)(2,1)S(1)} %copy-done, s32[4096]{0:T(1024)S(1)} %fusion.29), kind=kCustom, calls=%fused_computation | custom fusion | bytes 4210688 | tf_op jit(solution)/shard_map/gather | solution.py:48
  22.7 1.7 broadcast_select_fusion
  24.4 0.0 copy-start.1
  24.4 16.9 %all-to-all-start = ((bf16[32,128,256]{2,1,0:T(8,128)(2,1)}), bf16[32,128,256]{2,1,0:T(8,128)(2,1)S(1)}, u32[]{:S(2)}, u32[]{:S(2)}) async-start(bf16[32,128,256]{2,1,0:T(8,128)(2,1)} %broadcast_select_fusion), calls=%async_computation | async-start | bytes 4194304 | tf_op jit(solution)/shard_map/all_to_all | solution.py:49
  41.2 0.0 copy-start.5
  41.3 0.0 copy-start.2
  41.3 0.0 all-gather.3.cloned.1.call-start
  41.3 0.0 copy-done.1
  41.4 0.1 copy.9
  41.5 0.4 copy-done.5
  42.0 97.9 %all-to-all-done = bf16[32,128,256]{2,1,0:T(8,128)(2,1)S(1)} async-done(((bf16[32,128,256]{2,1,0:T(8,128)(2,1)}), bf16[32,128,256]{2,1,0:T(8,128)(2,1)S(1)}, u32[]{:S(2)}, u32[]{:S(2)}) %all-to-all-start) | async-done | bytes 2097184 | tf_op jit(solution)/shard_map/all_to_all | solution.py:49
  139.9 0.0 copy-done.2
  139.9 0.8 convolution_bitcast_fusion
  140.7 0.2 fusion.31
  140.8 0.1 copy.10
  141.0 0.1 copy.12
  141.1 0.0 copy-start.4
  141.1 0.1 copy.11
  141.2 0.3 fusion.14
  141.6 2.8 %collective-permute-start = (f32[38,1,128]{2,1,0:T(1,128)S(1)}, f32[38,1,128]{2,1,0:T(1,128)S(1)}, u32[]{:S(2)}, u32[]{:S(2)}) collective-permute-start(f32[38,1,128]{2,1,0:T(1,128)S(1)} %get-tuple-element.14), channel_id=1, source_target_pairs={{16,0},{32,16},{48,32},{64,48},{80,64},{96,80},{112,96},{128,112},... | collective-permute-start | bytes 58376 | tf_op jit(solution)/shard_map/ppermute | solution.py:23
  144.3 4.2 %collective-permute-start.1 = (f32[38,1,128]{2,1,0:T(1,128)S(1)}, f32[38,1,128]{2,1,0:T(1,128)S(1)}, u32[]{:S(2)}, u32[]{:S(2)}) collective-permute-start(f32[38,1,128]{2,1,0:T(1,128)S(1)} %get-tuple-element.15), channel_id=1, source_target_pairs={{0,16},{16,32},{32,48},{48,64},{64,80},{80,96},{96,112},{112,128},... | collective-permute-start | bytes 58376 | tf_op jit(solution)/shard_map/ppermute | solution.py:20
  148.6 0.0 copy-done.4
  148.6 0.0 collective-permute-done
  148.6 0.8 collective-permute-done.1
  149.4 0.5 fusion.3
  150.0 1.9 collective-permute-start.2
  151.9 4.2 %collective-permute-start.3 = (f32[38,1,128]{2,1,0:T(1,128)S(1)}, f32[38,1,128]{2,1,0:T(1,128)S(1)}, u32[]{:S(2)}, u32[]{:S(2)}) collective-permute-start(f32[38,1,128]{2,1,0:T(1,128)S(1)} %get-tuple-element.13), channel_id=1, source_target_pairs={{0,16},{16,32},{32,48},{48,64},{64,80},{80,96},{96,112},{112,128},... | collective-permute-start | bytes 58376 | tf_op jit(solution)/shard_map/ppermute | solution.py:20
  156.2 0.0 collective-permute-done.2
  156.2 0.9 collective-permute-done.3
  157.0 0.5 fusion.7
  157.6 1.9 collective-permute-start.4
  159.5 4.2 %collective-permute-start.5 = (f32[38,1,128]{2,1,0:T(1,128)S(1)}, f32[38,1,128]{2,1,0:T(1,128)S(1)}, u32[]{:S(2)}, u32[]{:S(2)}) collective-permute-start(f32[38,1,128]{2,1,0:T(1,128)S(1)} %get-tuple-element.11), channel_id=1, source_target_pairs={{0,16},{16,32},{32,48},{48,64},{64,80},{80,96},{96,112},{112,128},... | collective-permute-start | bytes 58376 | tf_op jit(solution)/shard_map/ppermute | solution.py:20
  163.8 0.0 collective-permute-done.4
  163.8 0.9 collective-permute-done.5
  164.6 0.6 fusion.12
  165.2 0.9 reshape.88
  166.1 0.0 all-gather.3.cloned.1.call-update
  166.2 0.0 copy-start.3
  166.2 69.0 %all-gather.3.cloned.1.call-done = bf16[16,38,4096]{2,1,0:T(8,128)(2,1)} async-done(((bf16[1,38,4096]{2,1,0:T(8,128)(2,1)}), bf16[16,38,4096]{2,1,0:T(8,128)(2,1)}) %all-gather.3.cloned.1.call-update) | async-done | bytes 4980752 | tf_op jit(solution)/shard_map/all_gather | solution.py:66
  235.2 5.7 %reshape.89 = bf16[608,4096]{1,0:T(8,128)(2,1)} reshape(bf16[16,38,4096]{2,1,0:T(8,128)(2,1)} %all-gather.3.cloned.1.call-done) | data formatting | bytes 9961472
  240.9 0.0 copy-done.3
  240.9 4.2 %convolution_bitcast_fusion.1 = f32[38,4096]{1,0:T(8,128)} fusion(bf16[608,4096]{1,0:T(8,128)(2,1)} %reshape.89, bf16[38,608]{1,0:T(8,128)(2,1)S(1)} %copy-done.3), kind=kOutput, calls=%fused_computation.2 | convolution fusion | flops 189267968 | bytes 5649536 | tf_op jit(solution)/shard_map/dot_general | solution.py:64
  (6 shorter events, 0.2 us)
Async XLA Ops:
  6.5 1.5 copy-start
  24.4 17.0 %copy-start.1 = (bf16[38,4096]{1,0:T(8,128)(2,1)S(1)}, bf16[38,4096]{1,0:T(8,128)(2,1)}, u32[]{:S(2)}) copy-start(bf16[38,4096]{1,0:T(8,128)(2,1)} %param.13) | copy-start | bytes 933892
  24.4 115.5 %all-to-all-start = ((bf16[32,128,256]{2,1,0:T(8,128)(2,1)}), bf16[32,128,256]{2,1,0:T(8,128)(2,1)S(1)}, u32[]{:S(2)}, u32[]{:S(2)}) async-start(bf16[32,128,256]{2,1,0:T(8,128)(2,1)} %broadcast_select_fusion), calls=%async_computation | async-start | bytes 4194304 | tf_op jit(solution)/shard_map/all_to_all | solution.py:49
  41.2 0.7 copy-start.5
  41.3 98.6 %copy-start.2 = (bf16[3,256,38]{1,2,0:T(8,128)(2,1)S(1)}, bf16[3,256,38]{1,2,0:T(8,128)(2,1)}, u32[]{:S(2)}) copy-start(bf16[3,256,38]{1,2,0:T(8,128)(2,1)} %param.12) | copy-start | bytes 175108
  41.3 193.9 %all-gather.3.cloned.1.call-start = ((), (), s32[]{:S(2)}) async-start(), calls=%async_computation.1 | async-start | bytes 5570560 | tf_op jit(solution)/shard_map/all_gather | solution.py:66
  141.1 7.5 %copy-start.4 = (f32[2,38]{1,0:T(2,128)S(1)}, f32[2,38]{1,0:T(2,128)}, u32[]{:S(2)}) copy-start(f32[2,38]{1,0:T(2,128)} %param.14) | copy-start | bytes 916
  141.6 7.0 %collective-permute-start = (f32[38,1,128]{2,1,0:T(1,128)S(1)}, f32[38,1,128]{2,1,0:T(1,128)S(1)}, u32[]{:S(2)}, u32[]{:S(2)}) collective-permute-start(f32[38,1,128]{2,1,0:T(1,128)S(1)} %get-tuple-element.14), channel_id=1, source_target_pairs={{16,0},{32,16},{48,32},{64,48},{80,64},{96,80},{112,96},{128,112},... | collective-permute-start | bytes 58376 | tf_op jit(solution)/shard_map/ppermute | solution.py:23
  144.3 5.1 %collective-permute-start.1 = (f32[38,1,128]{2,1,0:T(1,128)S(1)}, f32[38,1,128]{2,1,0:T(1,128)S(1)}, u32[]{:S(2)}, u32[]{:S(2)}) collective-permute-start(f32[38,1,128]{2,1,0:T(1,128)S(1)} %get-tuple-element.15), channel_id=1, source_target_pairs={{0,16},{16,32},{32,48},{48,64},{64,80},{80,96},{96,112},{112,128},... | collective-permute-start | bytes 58376 | tf_op jit(solution)/shard_map/ppermute | solution.py:20
  150.0 6.1 %collective-permute-start.2 = (f32[38,1,128]{2,1,0:T(1,128)S(1)}, f32[38,1,128]{2,1,0:T(1,128)S(1)}, u32[]{:S(2)}, u32[]{:S(2)}) collective-permute-start(f32[38,1,128]{2,1,0:T(1,128)S(1)} %get-tuple-element.12), channel_id=1, source_target_pairs={{16,0},{32,16},{48,32},{64,48},{80,64},{96,80},{112,96},{128,112},... | collective-permute-start | bytes 58376 | tf_op jit(solution)/shard_map/ppermute | solution.py:23
  151.9 5.1 %collective-permute-start.3 = (f32[38,1,128]{2,1,0:T(1,128)S(1)}, f32[38,1,128]{2,1,0:T(1,128)S(1)}, u32[]{:S(2)}, u32[]{:S(2)}) collective-permute-start(f32[38,1,128]{2,1,0:T(1,128)S(1)} %get-tuple-element.13), channel_id=1, source_target_pairs={{0,16},{16,32},{32,48},{48,64},{64,80},{80,96},{96,112},{112,128},... | collective-permute-start | bytes 58376 | tf_op jit(solution)/shard_map/ppermute | solution.py:20
  157.6 6.1 %collective-permute-start.4 = (f32[38,1,128]{2,1,0:T(1,128)S(1)}, f32[38,1,128]{2,1,0:T(1,128)S(1)}, u32[]{:S(2)}, u32[]{:S(2)}) collective-permute-start(f32[38,1,128]{2,1,0:T(1,128)S(1)} %get-tuple-element.10), channel_id=1, source_target_pairs={{16,0},{32,16},{48,32},{64,48},{80,64},{96,80},{112,96},{128,112},... | collective-permute-start | bytes 58376 | tf_op jit(solution)/shard_map/ppermute | solution.py:23
  159.5 5.1 %collective-permute-start.5 = (f32[38,1,128]{2,1,0:T(1,128)S(1)}, f32[38,1,128]{2,1,0:T(1,128)S(1)}, u32[]{:S(2)}, u32[]{:S(2)}) collective-permute-start(f32[38,1,128]{2,1,0:T(1,128)S(1)} %get-tuple-element.11), channel_id=1, source_target_pairs={{0,16},{16,32},{32,48},{48,64},{64,80},{80,96},{96,112},{112,128},... | collective-permute-start | bytes 58376 | tf_op jit(solution)/shard_map/ppermute | solution.py:20
  166.2 74.8 %copy-start.3 = (bf16[38,608]{1,0:T(8,128)(2,1)S(1)}, bf16[38,608]{1,0:T(8,128)(2,1)}, u32[]{:S(2)}) copy-start(bf16[38,608]{1,0:T(8,128)(2,1)} %param.15) | copy-start | bytes 138628
Sparse Core Ops, SparseCore 0:
  166.3 68.8 all-gather.2
where the time goes:
time: 253 us; the launch traced here: 252 us
  waiting for transfers between devices  170 us (67%)
  starting transfers between devices  36.2 us (14%)
  local copies, waits for them, and re-layouts  22.4 us (9%)
  between operations  13.6 us (5%)
  other arithmetic  5.22 us (2%)
  matrix products  4.96 us (2%)
    all_to_all x1, waiting for transfers between devices, on_device(): lax.all_to_all(outgoing, 'swath', split_axis=0, concat_axis=0, tiled=True)  97.9 us
    all_gather x1, waiting for transfers between devices, on_device(): lax.all_gather(smoothed, 'chan', axis=0, tiled=True)  69 us
    all_to_all x1, starting transfers between devices, on_device(): lax.all_to_all(outgoing, 'swath', split_axis=0, concat_axis=0, tiled=True)  16.9 us
    gather x1, local copies, waits for them, and re-layouts, on_device(): grid_profiles[slot_rows]  14.6 us
    ppermute x3, starting transfers between devices, extended_2(): lax.ppermute(lax.slice_in_dim(block, block.shape[dim] - width, None, axis...  12.6 us
    unnamed x18, local copies, waits for them, and re-layouts  7.56 us
    ppermute x3, starting transfers between devices, extended_2(): lax.ppermute(lax.slice_in_dim(block, 0, width, axis=dim), axis, backward)  6.62 us
  transfers between devices with their start and end apart: 8, of which 5 were waited for; matrix products, arithmetic and copies ran while one was open for 0% of the time, Pallas kernels for 0%

commit v1 on v0

v1 whole, which is shorter than its diff:
```python
import math

import jax
import jax.numpy as jnp
from jax import lax
from jax.sharding import PartitionSpec as P

XTRACK = 128
NANG = 8
SWEEPS = 3

max_zenith = math.pi / 3.0


def edge_lines(block, width):
    count = lax.axis_size("swath")
    forward = [(i, i + 1) for i in range(count - 1)]
    backward = [(target, source) for source, target in forward]
    low = lax.ppermute(block[:, -width:], "swath", forward)
    high = lax.ppermute(block[:, :width], "swath", backward)
    return jnp.concatenate([low, block, high], axis=1)


def diffuse_once(extended, along_rate, cross_rate):
    center = extended[:, 1:-1]
    along_sum = extended[:, 2:] + extended[:, :-2] - 2.0 * center
    side_pad = jnp.pad(center, ((0, 0), (0, 0), (1, 1)))
    cross_sum = side_pad[:, :, 2:] + side_pad[:, :, :-2] - 2.0 * center
    return center + along_rate * along_sum + cross_rate * cross_sum


def on_device(grid_profiles, send_lists, counts, angle_index, jacobian, observed, kappa, factor):
    members = lax.axis_size("chan")
    member = lax.axis_index("chan")
    swaths = lax.axis_size("swath")
    swath = lax.axis_index("swath")
    slots = send_lists.shape[2]
    share = slots // members
    own_chan = observed.shape[0]
    pixel_count = observed.shape[1]
    line_count = pixel_count // XTRACK
    depth = grid_profiles.shape[1]

    rows = lax.dynamic_slice_in_dim(send_lists[0], member * share, share, axis=1)
    slot = member * share + jnp.arange(share, dtype=jnp.int32)
    live_slot = slot[None, :] < counts[0][:, None]
    zero_value = jnp.zeros((), grid_profiles.dtype)
    outgoing = jnp.where(live_slot[:, :, None], grid_profiles[rows], zero_value)
    incoming = lax.all_to_all(outgoing, "swath", split_axis=0, concat_axis=0, tiled=True)
    gathered = lax.all_gather(incoming, "chan", axis=0, tiled=False)
    pixel_profiles = gathered.transpose(1, 0, 2, 3).reshape(pixel_count, depth)
    whole_factor = lax.all_gather(factor, "chan", axis=0, tiled=True)

    model = jnp.einsum("mkc,pk->mcp", jacobian, pixel_profiles, preferred_element_type=jnp.float32)
    zenith = angle_index.astype(jnp.float32) * (max_zenith / (NANG - 1))
    slant_path = 1.0 / jnp.cos(zenith) - 1.0
    model = model.reshape(3, own_chan, line_count, XTRACK)
    departure = observed.astype(jnp.float32).reshape(own_chan, line_count, XTRACK) - (
        model[0] + slant_path * model[1] + slant_path * slant_path * model[2]
    )
    along_rate = kappa[0][:, None, None]
    cross_rate = kappa[1][:, None, None]
    field = edge_lines(departure, SWEEPS)
    line = swath * line_count - SWEEPS + jnp.arange(line_count + 2 * SWEEPS, dtype=jnp.int32)
    inside = (line >= 0) & (line < swaths * line_count)
    for sweep in range(SWEEPS):
        field = diffuse_once(field, along_rate, cross_rate)
        kept = inside[sweep + 1 : inside.shape[0] - sweep - 1]
        field = jnp.where(kept[None, :, None], field, 0.0)
    smoothed = field.reshape(own_chan, pixel_count).astype(jnp.bfloat16)
    every_channel = lax.all_to_all(smoothed, "chan", split_axis=1, concat_axis=0, tiled=True)
    weighted = jnp.dot(whole_factor, every_channel, preferred_element_type=jnp.float32)
    return lax.all_to_all(weighted, "chan", split_axis=0, concat_axis=1, tiled=True)


def solution(mesh):
    in_specs = (
        P("swath", None),
        P("swath", None, None),
        P("swath", None),
        P(),
        P(None, None, "chan"),
        P("chan", "swath"),
        P(None, "chan"),
        P("chan", None),
    )
    out_specs = P("chan", "swath")
    return jax.shard_map(
        on_device, mesh=mesh, in_specs=in_specs, out_specs=out_specs, check_vma=False
    )
```

time: 253 us -> 164 us (0.65)
  the two profiles are of different devices: /device:TPU:1 before, /device:TPU:96 now
where the time goes in v1:
time: 164 us
  blocking collectives  71 us (43%)
  waiting for transfers between devices  56.1 us (34%)
  between operations  13.7 us (8%)
  starting transfers between devices  10.5 us (6%)
  local copies, waits for them, and re-layouts  7.18 us (4%)
  other arithmetic  4.24 us (3%)
    all_gather x1, waiting for transfers between devices, on_device(): gathered = lax.all_gather(incoming, 'chan', axis=0, tiled=False)  54.3 us
    all_to_all x1, blocking collectives, on_device(): lax.all_to_all(outgoing, 'swath', split_axis=0, concat_axis=0, tiled=True)  28.5 us
    all_gather x1, blocking collectives, on_device(): whole_factor = lax.all_gather(factor, 'chan', axis=0, tiled=True)  25.8 us
    all_to_all x1, blocking collectives, on_device(): lax.all_to_all(weighted, 'chan', split_axis=0, concat_axis=1, tiled=True)  16.7 us
    all_to_all x1, starting transfers between devices, on_device(): lax.all_to_all(smoothed, 'chan', split_axis=1, concat_axis=0, tiled=True)  4.94 us
    ppermute x1, starting transfers between devices, edge_lines(): high = lax.ppermute(block[:, :width], 'swath', backward)  3.64 us
  transfers between devices with their start and end apart: 4, of which 2 were waited for; matrix products, arithmetic and copies ran while one was open for 0% of the time, Pallas kernels for 0%

profile of v1, /device:TPU:96, one launch (start us, length us, event | category | flops | bytes accessed | tf_op | source)
XLA Modules:
  0.0 163.9 jit_solution(3897559961001162474)
XLA Ops:
  6.5 0.0 copy-start
  6.5 0.0 copy-start.1
  6.5 0.0 all-gather.4.cloned.1.call-start
  6.5 0.9 compare_select_fusion
  7.4 0.1 reshape.103
  7.5 0.1 copy-done
  7.6 0.0 copy-start.5
  7.6 0.0 copy-start.4
  7.6 1.1 gather_fusion
  8.7 0.7 broadcast_compare_fusion
  9.5 0.1 bitcast_select_fusion
  9.6 28.5 %all_to_all.40 = bf16[32,8,256]{2,1,0:T(8,128)(2,1)} all-to-all(bf16[32,8,256]{2,1,0:T(8,128)(2,1)S(1)} %bitcast_select_fusion), channel_id=1, replica_groups=mesh['swath'=32,'chan'=16] {'swath'}, dimensions={0} | all-to-all | bytes 262144 | tf_op jit(solution)/shard_map/all_to_all | solution.py:49
  38.1 0.0 all-gather.4.cloned.1.call-update
  38.1 0.0 copy-done.1
  38.2 0.1 copy.18
  38.3 0.0 copy-done.5
  38.4 0.0 copy-done.4
  38.4 54.3 %all-gather.4.cloned.1.call-done = bf16[512,8,256]{2,1,0:T(8,128)(2,1)} async-done(((bf16[32,8,256]{2,1,0:T(8,128)(2,1)}), bf16[512,8,256]{2,1,0:T(8,128)(2,1)}) %all-gather.4.cloned.1.call-update) | async-done | bytes 2097168 | tf_op jit(solution)/shard_map/all_gather | solution.py:50
  92.7 0.0 copy-start.2
  92.7 1.8 %copy.15 = bf16[32,16,8,256]{3,2,1,0:T(8,128)(2,1)S(1)} copy(bf16[32,16,8,256]{3,2,0,1:T(8,128)(2,1)} %bitcast.57) | data formatting | bytes 4194304 | tf_op jit(solution)/shard_map/transpose | solution.py:51
  94.6 0.0 copy-done.2
  94.6 0.8 convolution_bitcast_fusion
  95.4 0.2 fusion.29
  95.6 0.1 copy.19
  95.7 0.1 copy.20
  95.9 0.1 copy.21
  96.0 0.3 fusion.23
  96.3 1.9 %collective-permute-start = (f32[38,3,128]{2,1,0:T(4,128)S(1)}, f32[38,3,128]{2,1,0:T(4,128)S(1)}, u32[]{:S(2)}, u32[]{:S(2)}) collective-permute-start(f32[38,3,128]{2,1,0:T(4,128)S(1)} %get-tuple-element.10), channel_id=1, source_target_pairs={{0,16},{16,32},{32,48},{48,64},{64,80},{80,96},{96,112},{112,128},... | collective-permute-start | bytes 175112 | tf_op jit(solution)/shard_map/ppermute | solution.py:19
  98.2 3.6 %collective-permute-start.1 = (f32[38,3,128]{2,1,0:T(4,128)S(1)}, f32[38,3,128]{2,1,0:T(4,128)S(1)}, u32[]{:S(2)}, u32[]{:S(2)}) collective-permute-start(f32[38,3,128]{2,1,0:T(4,128)S(1)} %get-tuple-element.11), channel_id=1, source_target_pairs={{16,0},{32,16},{48,32},{64,48},{80,64},{96,80},{112,96},{128,112},... | collective-permute-start | bytes 175112 | tf_op jit(solution)/shard_map/ppermute | solution.py:20
  101.9 0.1 slice.80
  102.0 0.1 slice.79
  102.1 0.1 slice.78
  102.1 0.0 collective-permute-done
  102.1 1.8 %collective-permute-done.1 = f32[38,3,128]{2,1,0:T(4,128)S(1)} collective-permute-done((f32[38,3,128]{2,1,0:T(4,128)S(1)}, f32[38,3,128]{2,1,0:T(4,128)S(1)}, u32[]{:S(2)}, u32[]{:S(2)}) %collective-permute-start.1) | collective-permute-done | bytes 58400 | tf_op jit(solution)/shard_map/ppermute | solution.py:20
  103.9 0.1 pad_maximum_fusion
  104.0 0.1 slice.110
  104.1 0.7 fusion.4
  104.8 0.1 slice.113
  104.8 0.7 fusion.9
  105.5 0.1 slice.116
  105.6 0.0 copy-start.3
  105.6 0.7 fusion.21
  106.3 0.1 convert_element_type.19
  106.4 0.8 copy.16
  107.2 4.9 %all-to-all-start.1 = ((bf16[38,16,256]{2,0,1:T(8,128)(2,1)}), bf16[38,16,256]{2,0,1:T(8,128)(2,1)S(1)}, u32[]{:S(2)}, u32[]{:S(2)}) async-start(bf16[38,16,256]{2,0,1:T(8,128)(2,1)} %copy.16), calls=%async_computation.1 | async-start | bytes 655360 | tf_op jit(solution)/shard_map/all_to_all | solution.py:71
  112.1 0.0 copy-done.3
  112.2 25.8 %all-gather.1 = bf16[16,38,608]{2,1,0:T(8,128)(2,1)S(1)} all-gather(bf16[1,38,608]{2,1,0:T(8,128)(2,1)S(1)} %bitcast.59), channel_id=1, replica_groups=mesh['swath'=32,'chan'=16] {'chan'}, dimensions={0}, use_global_device_ids=true | all-gather | bytes 785536 | tf_op jit(solution)/shard_map/all_gather | solution.py:52
  137.9 0.4 reshape.112
  138.3 0.0 all-to-all-done.1
  138.3 0.1 all_to_all.32
  138.4 0.4 convolution_bitcast_fusion.1
  138.8 0.1 all_to_all.33
  138.9 16.7 %all_to_all.41 = f32[16,38,256]{2,1,0:T(8,128)S(1)} all-to-all(f32[16,38,256]{2,1,0:T(8,128)S(1)} %all_to_all.33), channel_id=1, replica_groups=mesh['swath'=32,'chan'=16] {'chan'}, dimensions={0} | all-to-all | bytes 1245184 | tf_op jit(solution)/shard_map/all_to_all | solution.py:73
  155.6 0.2 copy.17
  155.9 1.2 copy.22
  (8 shorter events, 0.2 us)
Async XLA Ops:
  6.5 1.1 copy-start
  6.5 31.6 %copy-start.1 = (bf16[38,4096]{1,0:T(8,128)(2,1)S(1)}, bf16[38,4096]{1,0:T(8,128)(2,1)}, u32[]{:S(2)}) copy-start(bf16[38,4096]{1,0:T(8,128)(2,1)} %param.13) | copy-start | bytes 933892
  6.5 86.2 %all-gather.4.cloned.1.call-start = ((), (), s32[]{:S(2)}) async-start(), calls=%async_computation.3 | async-start | bytes 2228224 | tf_op jit(solution)/shard_map/all_gather | solution.py:50
  7.6 30.7 %copy-start.5 = (s32[128]{0:T(128)S(1)}, s32[128]{0:T(128)}, u32[]{:S(2)}) copy-start(s32[128]{0:T(128)} %param.11) | copy-start | bytes 1540
  7.6 30.8 %copy-start.4 = (f32[2,38]{1,0:T(2,128)S(1)}, f32[2,38]{1,0:T(2,128)}, u32[]{:S(2)}) copy-start(f32[2,38]{1,0:T(2,128)} %param.14) | copy-start | bytes 916
  92.7 1.9 %copy-start.2 = (bf16[3,256,38]{1,2,0:T(8,128)(2,1)S(1)}, bf16[3,256,38]{1,2,0:T(8,128)(2,1)}, u32[]{:S(2)}) copy-start(bf16[3,256,38]{1,2,0:T(8,128)(2,1)} %param.12) | copy-start | bytes 175108
  96.3 5.8 %collective-permute-start = (f32[38,3,128]{2,1,0:T(4,128)S(1)}, f32[38,3,128]{2,1,0:T(4,128)S(1)}, u32[]{:S(2)}, u32[]{:S(2)}) collective-permute-start(f32[38,3,128]{2,1,0:T(4,128)S(1)} %get-tuple-element.10), channel_id=1, source_target_pairs={{0,16},{16,32},{32,48},{48,64},{64,80},{80,96},{96,112},{112,128},... | collective-permute-start | bytes 175112 | tf_op jit(solution)/shard_map/ppermute | solution.py:19
  98.2 5.6 %collective-permute-start.1 = (f32[38,3,128]{2,1,0:T(4,128)S(1)}, f32[38,3,128]{2,1,0:T(4,128)S(1)}, u32[]{:S(2)}, u32[]{:S(2)}) collective-permute-start(f32[38,3,128]{2,1,0:T(4,128)S(1)} %get-tuple-element.11), channel_id=1, source_target_pairs={{16,0},{32,16},{48,32},{64,48},{80,64},{96,80},{112,96},{128,112},... | collective-permute-start | bytes 175112 | tf_op jit(solution)/shard_map/ppermute | solution.py:20
  105.6 6.5 %copy-start.3 = (bf16[38,608]{1,0:T(8,128)(2,1)S(1)}, bf16[38,608]{1,0:T(8,128)(2,1)}, u32[]{:S(2)}) copy-start(bf16[38,608]{1,0:T(8,128)(2,1)} %param.15) | copy-start | bytes 138628
  107.2 31.1 %all-to-all-start.1 = ((bf16[38,16,256]{2,0,1:T(8,128)(2,1)}), bf16[38,16,256]{2,0,1:T(8,128)(2,1)S(1)}, u32[]{:S(2)}, u32[]{:S(2)}) async-start(bf16[38,16,256]{2,0,1:T(8,128)(2,1)} %copy.16), calls=%async_computation.1 | async-start | bytes 655360 | tf_op jit(solution)/shard_map/all_to_all | solution.py:71
Sparse Core Ops, SparseCore 0:
  38.2 54.4 all-gather.3

commit v2 on v0

v2 whole, which is shorter than its diff:
```python
import functools
import math

import jax
import jax.numpy as jnp
from jax import lax
from jax.experimental import pallas as pl
from jax.experimental.pallas import tpu as pltpu
from jax.sharding import PartitionSpec as P

XTRACK = 128
NANG = 8
SWEEPS = 3
SIDE = 4
MEMBERS = SIDE * SIDE
SWATHS = 2 * MEMBERS
LINES = 32
DEPTH = 256
PADDED = 48
GROUP = 4
MESH = pl.DeviceIdType.MESH

max_zenith = math.pi / 3.0


def kernel(
    own_chan,
    outgoing,
    own_factor,
    jac,
    observed,
    slant,
    rates,
    out,
    profiles,
    factor,
    field,
    field_1,
    field_2,
    smoothed,
    every,
    product,
    arrived,
    slot_send,
    slot_recv,
    slot_local,
    ring_send,
    ring_recv,
    edge_send,
    edge_recv,
    there_send,
    there_recv,
    back_send,
    back_recv,
):
    swath = lax.axis_index("swath")
    chan = lax.axis_index("chan")
    x, y = chan // SIDE, chan % SIDE
    above = lax.rem(swath + 1, SWATHS)
    below = lax.rem(swath + SWATHS - 1, SWATHS)

    def member(route, first, second):
        dx, dy = (first, second) if route == 0 else (second, first)
        return lax.rem(x + dx + SIDE, SIDE) * SIDE + lax.rem(y + dy + SIDE, SIDE)

    def line_of(route, who):
        return lax.rem(who + SWATHS - swath, MEMBERS) + MEMBERS * route

    partners = [line_of(k, chan) for k in range(2)]

    barrier = pltpu.get_barrier_semaphore()
    for i in range(1, MEMBERS):
        other = lax.rem(chan + i, MEMBERS)
        pl.semaphore_signal(barrier, inc=1, device_id={"chan": other}, device_id_type=MESH)
    for other in (above, below):
        pl.semaphore_signal(barrier, inc=1, device_id={"swath": other}, device_id_type=MESH)
    for other in partners:

        @pl.when(other != swath)
        def _():
            pl.semaphore_signal(barrier, inc=1, device_id={"swath": other}, device_id_type=MESH)

    distinct = sum(jnp.where(other != swath, 1, 0) for other in partners)
    pl.semaphore_wait(barrier, MEMBERS + 1 + distinct)

    def slot_copy(k):
        return pltpu.make_async_remote_copy(
            src_ref=outgoing.at[k],
            dst_ref=profiles.at[swath],
            send_sem=slot_send.at[k],
            recv_sem=slot_recv.at[k],
            device_id={"swath": partners[k]},
            device_id_type=MESH,
        )

    def slot_kept(k):
        return pltpu.make_async_copy(outgoing.at[k], profiles.at[swath], slot_local.at[k])

    def slot_sent(k):
        half = swath // MEMBERS
        return pltpu.make_async_remote_copy(
            src_ref=outgoing.at[k],
            dst_ref=profiles.at[swath],
            send_sem=slot_send.at[k],
            recv_sem=slot_recv.at[half],
            device_id={"swath": partners[k]},
            device_id_type=MESH,
        )

    for k in range(2):

        @pl.when(partners[k] != swath)
        def _():
            slot_sent(k).start()

        @pl.when(partners[k] == swath)
        def _():
            slot_kept(k).start()

    def profile_piece(route, who):
        return profiles.at[line_of(route, who)]

    def profile_half(route, who, half):
        rows = XTRACK // 2
        return profiles.at[line_of(route, who), pl.ds(half * rows, rows)]

    def factor_piece(route, who):
        return factor.at[route, who]

    def factor_half(route, who, half):
        return factor.at[route, who, pl.ds(0, 32) if half == 0 else pl.ds(32, 16)]

    sent = []
    offsets = (0, -1, 1, 2)

    class Ring:
        def __init__(self, kind, route, piece, half):
            self.kind, self.route, self.piece, self.half = kind, route, piece, half
            self.copies = {}

        def send(self, key, number, source, target, to):
            at = (self.kind * 2 + self.route) * 20 + number
            copy = pltpu.make_async_remote_copy(
                src_ref=source,
                dst_ref=target,
                send_sem=ring_send.at[at],
                recv_sem=ring_recv.at[at],
                device_id={"chan": to},
                device_id_type=MESH,
            )
            copy.start()
            sent.append(copy)
            self.copies[key] = copy

        def whole(self, offset, source=None):
            who = member(self.route, offset, 0)
            target = self.piece(self.route, who)
            for way in range(2):
                to = member(self.route, 0, 1 - 2 * way)
                number = 4 + offsets.index(offset) * 2 + way
                self.send(("b", offset, way), number, target if source is None else source, target, to)

        def open(self, source=None):
            target = self.piece(self.route, chan)
            for way in range(2):
                to = member(self.route, 1 - 2 * way, 0)
                self.send(("a", way), way, target if source is None else source, target, to)
            self.whole(0, source)

        def relay(self):
            for way in range(2):
                self.copies["a", way].wait_recv()
                came = 2 * way - 1
                part = self.half(self.route, member(self.route, came, 0), way)
                self.send(("c", way), 2 + way, part, part, member(self.route, -came, 0))
                self.whole(came)

        def across(self):
            for way in range(2):
                self.copies["c", way].wait_recv()
            self.whole(2)

        def finish(self):
            for index, offset in enumerate(offsets):
                for way in range(2):
                    self.copies["b", offset, way].wait_recv()
                    came = 2 * way - 1
                    part = self.half(self.route, member(self.route, offset, came), way)
                    number = 12 + index * 2 + way
                    self.send(("d", offset, way), number, part, part, member(self.route, 0, -came))

        def close(self):
            for offset in offsets:
                for way in range(2):
                    self.copies["d", offset, way].wait_recv()

    profile_rings = [Ring(0, k, profile_piece, profile_half) for k in range(2)]
    factor_rings = [Ring(1, k, factor_piece, factor_half) for k in range(2)]

    for k, ring in enumerate(factor_rings):
        ring.open(own_factor.at[k])
    for k in range(2):
        factor[k, chan] = own_factor[k]
    for ring in factor_rings:
        ring.relay()
    for ring in factor_rings:
        ring.across()
    for k, ring in enumerate(profile_rings):

        @pl.when(partners[k] != swath)
        def _():
            slot_copy(k).wait_recv()

        @pl.when(partners[k] == swath)
        def _():
            slot_kept(k).wait()

        ring.open()
    for ring in factor_rings:
        ring.finish()
    for ring in profile_rings:
        ring.relay()
    for ring in profile_rings:
        ring.across()
    for ring in profile_rings:
        ring.finish()
    for ring in factor_rings:
        ring.close()
    for ring in profile_rings:
        ring.close()

    path = slant[...]
    path_2 = path * path

    def depart(group):
        start = group * GROUP
        rows = profiles[pl.ds(start, GROUP)].reshape(GROUP * XTRACK, DEPTH)
        model = lax.dot_general(
            jac[...], rows, (((1,), (1,)), ((), ())), preferred_element_type=jnp.float32
        )
        for i in range(GROUP):
            part = model[:, i * XTRACK : (i + 1) * XTRACK]
            columns = pl.ds(pl.multiple_of((start + i) * XTRACK, XTRACK), XTRACK)
            field[start + i + SWEEPS] = observed[:, columns].astype(jnp.float32) - (
                part[:PADDED]
                + path * part[PADDED : 2 * PADDED]
                + path_2 * part[2 * PADDED :]
            )

    depart(LINES // GROUP - 1)
    depart(0)
    depart(1)
    edges = []
    for way, (source, target, to) in enumerate(
        ((LINES, 0, above), (SWEEPS, LINES + SWEEPS, below))
    ):
        copy = pltpu.make_async_remote_copy(
            src_ref=field.at[pl.ds(source, SWEEPS)],
            dst_ref=field.at[pl.ds(target, SWEEPS)],
            send_sem=edge_send.at[way],
            recv_sem=edge_recv.at[way],
            device_id={"swath": to},
            device_id_type=MESH,
        )
        copy.start()
        edges.append(copy)
        sent.append(copy)

    @pl.loop(2, LINES // GROUP - 1)
    def _(group):
        depart(group)

    for copy in edges:
        copy.wait_recv()

    def clear(block, width):
        @pl.when(swath == 0)
        def _():
            block[pl.ds(0, width)] = jnp.zeros((width, PADDED, XTRACK), jnp.float32)

        @pl.when(swath == SWATHS - 1)
        def _():
            block[pl.ds(LINES + width, width)] = jnp.zeros((width, PADDED, XTRACK), jnp.float32)

    along_rate = rates[0]
    cross_rate = rates[1]
    column = lax.broadcasted_iota(jnp.int32, (PADDED, XTRACK), 1)

    def diffuse(block, at):
        center = block[at]
        along_sum = block[at + 1] + block[at - 1] - 2.0 * center
        left = jnp.where(column == 0, 0.0, pltpu.roll(center, 1, 1))
        right = jnp.where(column == XTRACK - 1, 0.0, pltpu.roll(center, XTRACK - 1, 1))
        cross_sum = right + left - 2.0 * center
        return center + along_rate * along_sum + cross_rate * cross_sum

    clear(field, 3)

    @pl.loop(0, (LINES + 4) // 2)
    def _(pair):
        for i in range(2):
            field_1[2 * pair + i] = diffuse(field, 2 * pair + i + 1)

    clear(field_1, 2)

    @pl.loop(0, (LINES + 2) // 2)
    def _(pair):
        for i in range(2):
            field_2[2 * pair + i] = diffuse(field_1, 2 * pair + i + 1)

    clear(field_2, 1)

    def there(who, into):
        return pltpu.make_async_remote_copy(
            src_ref=smoothed.at[pl.ds(2 * who, 2)],
            dst_ref=every.at[:, into],
            send_sem=there_send.at[who],
            recv_sem=there_recv.at[into],
            device_id={"chan": who},
            device_id_type=MESH,
        )

    def smooth_pair(i):
        who = lax.rem(chan + 1 + i, MEMBERS)
        for j in range(2):
            smoothed[2 * who + j] = diffuse(field_2, 2 * who + j + 1).astype(jnp.bfloat16)

    smooth_pair(0)

    @pl.loop(1, MEMBERS)
    def _(i):
        smooth_pair(i)
        there(lax.rem(chan + i, MEMBERS), chan).start()

    for j in range(2):
        every[j, chan] = smoothed[2 * chan + j]

    @pl.loop(1, MEMBERS)
    def _(i):
        who = lax.rem(chan + i, MEMBERS)
        there(who, who).wait_recv()

    pieces = [every[j].reshape(MEMBERS * PADDED, XTRACK) for j in range(2)]
    wide = jnp.concatenate(pieces, axis=1)
    half_depth = MEMBERS * PADDED // 2

    def weigh(group):
        rows = [
            factor[k, pl.ds(group * GROUP, GROUP)].reshape(GROUP * PADDED, half_depth)
            for k in range(2)
        ]
        block = jnp.dot(
            rows[0], wide[:half_depth], preferred_element_type=jnp.float32
        ) + jnp.dot(rows[1], wide[half_depth:], preferred_element_type=jnp.float32)
        for j in range(2):
            part = block[:, j * XTRACK : (j + 1) * XTRACK].astype(jnp.bfloat16)
            product[j, pl.ds(group * GROUP, GROUP)] = part.reshape(GROUP, PADDED, XTRACK)

    for group in range(MEMBERS // GROUP):
        weigh(group)

    def back(who, into):
        return pltpu.make_async_remote_copy(
            src_ref=product.at[:, who],
            dst_ref=arrived.at[pl.ds(2 * into, 2)],
            send_sem=back_send.at[who],
            recv_sem=back_recv.at[into],
            device_id={"chan": who},
            device_id_type=MESH,
        )

    @pl.loop(1, MEMBERS)
    def _(i):
        back(lax.rem(chan + i, MEMBERS), chan).start()

    for j in range(2):
        arrived[2 * chan + j] = product[j, chan]

    def settle(who):
        for j in range(2):
            at = 2 * who + j
            columns = pl.ds(pl.multiple_of(at * XTRACK, XTRACK), XTRACK)
            out[:, columns] = arrived[at].astype(jnp.float32)[:own_chan]

    settle(chan)

    @pl.loop(1, MEMBERS)
    def _(i):
        who = lax.rem(chan + i, MEMBERS)
        back(who, who).wait_recv()
        settle(who)

    for copy in sent:
        copy.wait_send()
    for k in range(2):

        @pl.when(partners[k] != swath)
        def _():
            slot_copy(k).wait_send()

    @pl.loop(1, MEMBERS)
    def _(i):
        who = lax.rem(chan + i, MEMBERS)
        there(who, chan).wait_send()
        back(who, chan).wait_send()


def on_device(grid_profiles, send_lists, counts, angle_index, jacobian, observed, kappa, factor):
    chan = lax.axis_index("chan")
    swath = lax.axis_index("swath")
    slots = send_lists.shape[2]
    own_chan = observed.shape[0]
    pixel_count = observed.shape[1]
    spare = PADDED - own_chan

    first = (chan - swath) % MEMBERS
    rows = send_lists[0].reshape(2, MEMBERS, slots)[:, first]
    live = counts[0].reshape(2, MEMBERS)[:, first]
    live_slot = jnp.arange(slots, dtype=jnp.int32)[None, :] < live[:, None]
    zero_value = jnp.zeros((), grid_profiles.dtype)
    outgoing = jnp.where(live_slot[:, :, None], grid_profiles[rows], zero_value)

    zenith = angle_index.astype(jnp.float32) * (max_zenith / (NANG - 1))
    slant_path = (1.0 / jnp.cos(zenith) - 1.0)[None, :]
    jac = jnp.pad(jacobian.transpose(0, 2, 1), ((0, 0), (0, spare), (0, 0)))
    jac = jac.reshape(3 * PADDED, DEPTH)
    padded = jnp.pad(observed, ((0, spare), (0, 0)))
    rates = jnp.broadcast_to(
        jnp.pad(kappa, ((0, 0), (0, spare)))[:, :, None], (2, PADDED, XTRACK)
    )
    own_factor = jnp.pad(
        factor.reshape(own_chan, MEMBERS, own_chan), ((0, spare), (0, 0), (0, spare))
    )
    half_depth = MEMBERS * PADDED // 2
    own_factor = own_factor.reshape(PADDED, 2, half_depth).transpose(1, 0, 2)

    vmem = pl.BlockSpec(memory_space=pltpu.VMEM)
    dma = pltpu.SemaphoreType.DMA
    return pl.pallas_call(
        functools.partial(kernel, own_chan),
        out_shape=jax.ShapeDtypeStruct((own_chan, pixel_count), jnp.float32),
        in_specs=[vmem] * 6,
        out_specs=vmem,
        scratch_shapes=[
            pltpu.VMEM((LINES, XTRACK, DEPTH), jnp.bfloat16),
            pltpu.VMEM((2, MEMBERS, PADDED, half_depth), jnp.bfloat16),
            pltpu.VMEM((LINES + 6, PADDED, XTRACK), jnp.float32),
            pltpu.VMEM((LINES + 4, PADDED, XTRACK), jnp.float32),
            pltpu.VMEM((LINES + 2, PADDED, XTRACK), jnp.float32),
            pltpu.VMEM((LINES, PADDED, XTRACK), jnp.bfloat16),
            pltpu.VMEM((2, MEMBERS, PADDED, XTRACK), jnp.bfloat16),
            pltpu.VMEM((2, MEMBERS, PADDED, XTRACK), jnp.bfloat16),
            pltpu.VMEM((LINES, PADDED, XTRACK), jnp.bfloat16),
            dma((2,)),
            dma((2,)),
            dma((2,)),
            dma((80,)),
            dma((80,)),
            dma((2,)),
            dma((2,)),
            dma((MEMBERS,)),
            dma((MEMBERS,)),
            dma((MEMBERS,)),
            dma((MEMBERS,)),
        ],
        compiler_params=pltpu.CompilerParams(collective_id=0, has_side_effects=True),
    )(outgoing, own_factor, jac, padded, slant_path, rates)


def solution(mesh):
    in_specs = (
        P("swath", None),
        P("swath", None, None),
        P("swath", None),
        P(),
        P(None, None, "chan"),
        P("chan", "swath"),
        P(None, "chan"),
        P("chan", None),
    )
    out_specs = P("chan", "swath")
    return jax.shard_map(
        on_device, mesh=mesh, in_specs=in_specs, out_specs=out_specs, check_vma=False
    )
```

time: 253 us -> 81.8 us (0.32)
  waiting for transfers between devices: 170 us -> 0 us
  Pallas kernels: 0 us -> 69.7 us
  starting transfers between devices: 36.2 us -> 0 us
  local copies, waits for them, and re-layouts: 22.4 us -> 8 us
  between operations: 13.6 us -> 0.06 us
  matrix products: 4.96 us -> 0 us
    all_to_all x1 -> x0, waiting for transfers between devices: 97.9 us -> none  [on_device(): lax.all_to_all(outgoing, 'swath', split_axis=0, concat_axis=0, tiled=True)]
    pallas_call x0 -> x1, Pallas kernels: none -> 69.7 us  [on_device(): pl.pallas_call(functools.partial(kernel, own_chan), out_shape=jax.ShapeDt...]
    all_gather x1 -> x0, waiting for transfers between devices: 69 us -> none  [on_device(): lax.all_gather(smoothed, 'chan', axis=0, tiled=True)]
    ppermute x6 -> x0, starting transfers between devices: 19.3 us -> none  [the longest x3 12.6 us: extended_2(): lax.ppermute(lax.slice_in_dim(block, block.shape[dim] - width, None, axis...]
    all_to_all x1 -> x0, starting transfers between devices: 16.9 us -> none  [on_device(): lax.all_to_all(outgoing, 'swath', split_axis=0, concat_axis=0, tiled=True)]
    gather x1, local copies, waits for them, and re-layouts: 14.6 us -> 1.15 us  [on_device(): outgoing = jnp.where(live_slot[:, :, None], grid_profiles[rows], zero_value)]
    unnamed x18 -> x12, local copies, waits for them, and re-layouts: 7.56 us -> 2.55 us
    dot_general x2 -> x0, matrix products: 4.96 us -> none  [the longest x1 4.18 us: on_device(): jnp.dot(factor, lax.all_gather(smoothed, 'chan', axis=0, tiled=True), pre...]
  transfers between devices with their start and end apart: 8 -> 0, of which waited for: 5 -> 0; matrix products, arithmetic and copies ran while one was open for 0% -> 0% of each run, Pallas kernels for 0% -> 0%
where the time goes in v2:
time: 81.8 us; the launch traced here: 81.1 us
  Pallas kernels  69.7 us (85%)
  local copies, waits for them, and re-layouts  8 us (10%)
  other arithmetic  3.35 us (4%)
    pallas_call x1, Pallas kernels, on_device(): pl.pallas_call(functools.partial(kernel, own_chan), out_shape=jax.ShapeDt...  69.7 us
    unnamed x12, local copies, waits for them, and re-layouts  2.55 us

profile of v2, /device:TPU:1, one launch (start us, length us, event | category | flops | bytes accessed | tf_op | source)
XLA Modules:
  0.0 81.1 jit_solution(1182483672895860273)
XLA Ops:
  0.0 0.0 copy-start
  0.0 0.0 copy-start.2
  0.0 0.5 broadcast.56
  0.5 1.3 %reduce.5 = s32[32]{0:T(128)S(1)} reduce(s32[1,32]{1,0:T(1,128)} %param.10, s32[]{:T(128)} %broadcast.56), dimensions={0}, to_apply=%param.10.reduce_sub_computation.3 | reduce | bytes 260 | tf_op args[2]
  1.8 0.1 reshape_squeeze.6
  1.9 0.2 dynamic-slice_reduce_fusion
  2.1 0.1 iota_compare_fusion
  2.2 0.7 constant_dynamic-slice_fusion
  2.9 0.0 copy-start.4
  2.9 1.2 %add_bitcast_fusion.slant = f32[1,128]{1,0:T(1,128)} fusion(s32[128]{0:T(128)} %param.11), kind=kLoop, calls=%fused_computation.8 | loop fusion | flops 512 | bytes 1024 | tf_op jit(solution)/shard_map/broadcast_in_dim | solution.py:424
  4.1 0.0 copy-done.4
  4.1 0.7 broadcast_in_dim.27.rates
  4.8 0.0 copy-done.2
  4.8 0.6 pad.17
  5.4 0.0 copy-done
  5.4 1.2 %gather_fusion = bf16[256,256]{1,0:T(8,128)(2,1)S(1)} fusion(bf16[1024,256]{1,0:T(8,128)(2,1)S(1)} %copy-done, s32[1024]{0:T(1024)S(1)} %pad_clamp_fusion), kind=kCustom, calls=%fused_computation | custom fusion | bytes 263168 | tf_op jit(solution)/shard_map/gather | solution.py:421
  6.6 0.0 copy-start.3
  6.6 0.7 broadcast_select_fusion.outgoing
  7.4 0.1 copy-done.3
  7.4 0.3 reshape.60
  7.7 0.0 copy-start.1
  7.7 0.3 reshape.61
  8.0 0.6 copy.11
  8.7 0.0 copy-done.1
  8.7 0.8 pad.18.observed
  9.4 69.7 %shard_map.82 = f32[38,4096]{1,0:T(8,128)} custom-call(bf16[2,128,256]{2,1,0:T(8,128)(2,1)} %broadcast_select_fusion.outgoing, bf16[2,48,384]{2,1,0:T(8,128)(2,1)} %bitcast.14, bf16[144,256]{1,0:T(8,128)(2,1)} %bitcast.13, bf16[48,4096]{1,0:T(8,128)(2,1)} %pad.18.observed, f32[1,128]{1,0:T(1,128)} %add_bitcast_fusion.slant, f32[2,48,128]{2,1,0:T(8,128)} %broadcast_in_dim.27.rates), custom_call_target="tpu_custom_call" | custom-call | tf_op jit(solution)/shard_map/pallas_call | solution.py:439
  79.1 2.0 %copy.13 = f32[38,4096]{1,0:T(8,128)} copy(f32[38,4096]{1,0:T(8,128)} %shard_map.82) | data formatting | bytes 1245184
  (4 shorter events, 0.1 us)
Async XLA Ops:
  0.0 5.4 %copy-start = (bf16[1024,256]{1,0:T(8,128)(2,1)S(1)}, bf16[1024,256]{1,0:T(8,128)(2,1)}, u32[]{:S(2)}) copy-start(bf16[1024,256]{1,0:T(8,128)(2,1)} %param.8) | copy-start | bytes 1572868
  0.0 4.8 %copy-start.2 = (bf16[3,256,38]{1,2,0:T(8,128)(2,1)S(1)}, bf16[3,256,38]{1,2,0:T(8,128)(2,1)}, u32[]{:S(2)}) copy-start(bf16[3,256,38]{1,2,0:T(8,128)(2,1)} %param.12) | copy-start | bytes 175108
  2.9 1.2 %copy-start.4 = (f32[2,38]{1,0:T(2,128)S(1)}, f32[2,38]{1,0:T(2,128)}, u32[]{:S(2)}) copy-start(f32[2,38]{1,0:T(2,128)} %param.14) | copy-start | bytes 916
  6.6 0.8 copy-start.3
  7.7 1.0 %copy-start.1 = (bf16[38,4096]{1,0:T(8,128)(2,1)S(1)}, bf16[38,4096]{1,0:T(8,128)(2,1)}, u32[]{:S(2)}) copy-start(bf16[38,4096]{1,0:T(8,128)(2,1)} %param.13) | copy-start | bytes 933892

commit v3 on v2

--- a/solution.py
+++ b/solution.py
@@ -17,6 +17,7 @@
 LINES = 32
 DEPTH = 256
 PADDED = 48
+ROWS = 40
 GROUP = 4
 MESH = pl.DeviceIdType.MESH
 
@@ -25,13 +26,19 @@
 
 def kernel(
     own_chan,
+    grid,
+    lists,
+    counts,
+    angle,
+    jac_in,
+    observed,
+    kappa,
+    factor_in,
+    out,
     outgoing,
     own_factor,
     jac,
-    observed,
-    slant,
-    rates,
-    out,
+    weights,
     profiles,
     factor,
     field,
@@ -68,6 +75,7 @@
 
     partners = [line_of(k, chan) for k in range(2)]
 
+    field[...] = jnp.zeros(field.shape, jnp.float32)
     barrier = pltpu.get_barrier_semaphore()
     for i in range(1, MEMBERS):
         other = lax.rem(chan + i, MEMBERS)
@@ -79,6 +87,36 @@
         @pl.when(other != swath)
         def _():
             pl.semaphore_signal(barrier, inc=1, device_id={"swath": other}, device_id_type=MESH)
+
+    grid_rows = grid.shape[0]
+    slot = lax.broadcasted_iota(jnp.int32, (1, XTRACK), 1)
+    grid_row = lax.broadcasted_iota(jnp.int32, (grid_rows, XTRACK), 0)
+    for k in range(2):
+        picked = lists[pl.ds(partners[k], 1), :]
+        picked = jnp.where(slot < counts[0, partners[k]], picked, -1)
+        chosen = jnp.where(grid_row == picked, 1.0, 0.0).astype(jnp.bfloat16)
+        outgoing[k] = lax.dot_general(
+            chosen, grid[...], (((0,), (0,)), ((), ())), preferred_element_type=jnp.float32
+        ).astype(jnp.bfloat16)
+
+    channels = MEMBERS * own_chan
+    place = lax.broadcasted_iota(jnp.int32, (1, MEMBERS * PADDED), 1)
+    owner = sum(jnp.where(place >= m * PADDED, 1, 0) for m in range(1, MEMBERS))
+    target = jnp.where(place - owner * PADDED < own_chan, place - owner * (PADDED - own_chan), -1)
+    source_row = lax.broadcasted_iota(jnp.int32, (channels, MEMBERS * PADDED), 0)
+    spread = jnp.where(source_row == target, 1.0, 0.0).astype(jnp.bfloat16)
+    spaced = jnp.dot(factor_in[...], spread, preferred_element_type=jnp.float32)
+    spaced = spaced.astype(jnp.bfloat16)
+    half_depth = MEMBERS * PADDED // 2
+    own_factor[...] = jnp.zeros(own_factor.shape, jnp.bfloat16)
+    for k in range(2):
+        own_factor[k, pl.ds(0, own_chan)] = spaced[:, k * half_depth : (k + 1) * half_depth]
+
+    jac[...] = jnp.zeros(jac.shape, jnp.bfloat16)
+    for m in range(3):
+        jac[pl.ds(m * PADDED, own_chan)] = jac_in[m]
+
+    smoothed[...] = jnp.zeros(smoothed.shape, jnp.bfloat16)
 
     distinct = sum(jnp.where(other != swath, 1, 0) for other in partners)
     pl.semaphore_wait(barrier, MEMBERS + 1 + distinct)
@@ -224,32 +262,55 @@
         ring.across()
     for ring in profile_rings:
         ring.finish()
+    zenith = angle[...].astype(jnp.float32) * (max_zenith / (NANG - 1))
+    path = 1.0 / jnp.cos(zenith) - 1.0
+    path_2 = path * path
+
+    def depart(route, first, second):
+        line = line_of(route, member(route, first, second))
+        model = lax.dot_general(
+            jac[...], profiles[line], (((1,), (1,)), ((), ())), preferred_element_type=jnp.float32
+        )
+        columns = pl.ds(pl.multiple_of(line * XTRACK, XTRACK), XTRACK)
+        value = (
+            model[:PADDED]
+            + path * model[PADDED : 2 * PADDED]
+            + path_2 * model[2 * PADDED :]
+        )
+        field[line + SWEEPS, pl.ds(0, own_chan)] = (
+            observed[:, columns].astype(jnp.float32) - value[:own_chan]
+        )
+
+    @pl.loop(0, 3)
+    def _(i):
+        for route in range(2):
+            for first in offsets:
+                depart(route, first, i - 1)
+
     for ring in factor_rings:
         ring.close()
     for ring in profile_rings:
         ring.close()
-
-    path = slant[...]
-    path_2 = path * path
-
-    def depart(group):
-        start = group * GROUP
-        rows = profiles[pl.ds(start, GROUP)].reshape(GROUP * XTRACK, DEPTH)
-        model = lax.dot_general(
-            jac[...], rows, (((1,), (1,)), ((), ())), preferred_element_type=jnp.float32
-        )
-        for i in range(GROUP):
-            part = model[:, i * XTRACK : (i + 1) * XTRACK]
-            columns = pl.ds(pl.multiple_of((start + i) * XTRACK, XTRACK), XTRACK)
-            field[start + i + SWEEPS] = observed[:, columns].astype(jnp.float32) - (
-                part[:PADDED]
-                + path * part[PADDED : 2 * PADDED]
-                + path_2 * part[2 * PADDED :]
-            )
-
-    depart(LINES // GROUP - 1)
-    depart(0)
-    depart(1)
+    for route in range(2):
+        for first in offsets:
+            depart(route, first, 2)
+
+    column = lax.broadcasted_iota(jnp.int32, (ROWS, XTRACK), 1)
+    on_diagonal = lax.broadcasted_iota(jnp.int32, (ROWS, own_chan), 0) == (
+        lax.broadcasted_iota(jnp.int32, (ROWS, own_chan), 1)
+    )
+    spread_rates = [
+        jnp.broadcast_to(
+            jnp.sum(jnp.where(on_diagonal, kappa[pl.ds(k, 1), :], 0.0), axis=1, keepdims=True),
+            (ROWS, XTRACK),
+        )
+        for k in range(2)
+    ]
+    weights[0] = 1.0 - 2.0 * (spread_rates[0] + spread_rates[1])
+    weights[1] = spread_rates[0]
+    weights[2] = jnp.where(column == 0, 0.0, spread_rates[1])
+    weights[3] = jnp.where(column == XTRACK - 1, 0.0, spread_rates[1])
+
     edges = []
     for way, (source, target, to) in enumerate(
         ((LINES, 0, above), (SWEEPS, LINES + SWEEPS, below))
@@ -266,48 +327,45 @@
         edges.append(copy)
         sent.append(copy)
 
-    @pl.loop(2, LINES // GROUP - 1)
-    def _(group):
-        depart(group)
-
     for copy in edges:
         copy.wait_recv()
 
     def clear(block, width):
         @pl.when(swath == 0)
         def _():
-            block[pl.ds(0, width)] = jnp.zeros((width, PADDED, XTRACK), jnp.float32)
+            block[pl.ds(0, width)] = jnp.zeros((width, ROWS, XTRACK), jnp.float32)
 
         @pl.when(swath == SWATHS - 1)
         def _():
-            block[pl.ds(LINES + width, width)] = jnp.zeros((width, PADDED, XTRACK), jnp.float32)
-
-    along_rate = rates[0]
-    cross_rate = rates[1]
-    column = lax.broadcasted_iota(jnp.int32, (PADDED, XTRACK), 1)
+            block[pl.ds(LINES + width, width)] = jnp.zeros((width, ROWS, XTRACK), jnp.float32)
+
+    weight = [weights[k] for k in range(4)]
 
     def diffuse(block, at):
         center = block[at]
-        along_sum = block[at + 1] + block[at - 1] - 2.0 * center
-        left = jnp.where(column == 0, 0.0, pltpu.roll(center, 1, 1))
-        right = jnp.where(column == XTRACK - 1, 0.0, pltpu.roll(center, XTRACK - 1, 1))
-        cross_sum = right + left - 2.0 * center
-        return center + along_rate * along_sum + cross_rate * cross_sum
+        left = pltpu.roll(center, 1, 1)
+        right = pltpu.roll(center, XTRACK - 1, 1)
+        return (
+            weight[0] * center
+            + weight[1] * (block[at + 1] + block[at - 1])
+            + (weight[2] * left + weight[3] * right)
+        )
+
+    def sweep(source, target, count, step):
+        @pl.loop(0, count // step)
+        def _(turn):
+            for i in range(step):
+                target[step * turn + i] = diffuse(source, step * turn + i + 1)
+
+        for at in range(count - count % step, count):
+            target[at] = diffuse(source, at + 1)
 
     clear(field, 3)
 
-    @pl.loop(0, (LINES + 4) // 2)
-    def _(pair):
-        for i in range(2):
-            field_1[2 * pair + i] = diffuse(field, 2 * pair + i + 1)
-
+    sweep(field, field_1, LINES + 4, 6)
     clear(field_1, 2)
 
-    @pl.loop(0, (LINES + 2) // 2)
-    def _(pair):
-        for i in range(2):
-            field_2[2 * pair + i] = diffuse(field_1, 2 * pair + i + 1)
-
+    sweep(field_1, field_2, LINES + 2, 6)
     clear(field_2, 1)
 
     def there(who, into):
@@ -323,7 +381,8 @@
     def smooth_pair(i):
         who = lax.rem(chan + 1 + i, MEMBERS)
         for j in range(2):
-            smoothed[2 * who + j] = diffuse(field_2, 2 * who + j + 1).astype(jnp.bfloat16)
+            value = diffuse(field_2, 2 * who + j + 1).astype(jnp.bfloat16)
+            smoothed[2 * who + j, pl.ds(0, ROWS)] = value
 
     smooth_pair(0)
 
@@ -342,7 +401,6 @@
 
     pieces = [every[j].reshape(MEMBERS * PADDED, XTRACK) for j in range(2)]
     wide = jnp.concatenate(pieces, axis=1)
-    half_depth = MEMBERS * PADDED // 2
 
     def weigh(group):
         rows = [
@@ -380,7 +438,7 @@
         for j in range(2):
             at = 2 * who + j
             columns = pl.ds(pl.multiple_of(at * XTRACK, XTRACK), XTRACK)
-            out[:, columns] = arrived[at].astype(jnp.float32)[:own_chan]
+            out[:, columns] = arrived[at, pl.ds(0, own_chan)]
 
     settle(chan)
 
@@ -406,47 +464,26 @@
 
 
 def on_device(grid_profiles, send_lists, counts, angle_index, jacobian, observed, kappa, factor):
-    chan = lax.axis_index("chan")
-    swath = lax.axis_index("swath")
-    slots = send_lists.shape[2]
     own_chan = observed.shape[0]
     pixel_count = observed.shape[1]
-    spare = PADDED - own_chan
-
-    first = (chan - swath) % MEMBERS
-    rows = send_lists[0].reshape(2, MEMBERS, slots)[:, first]
-    live = counts[0].reshape(2, MEMBERS)[:, first]
-    live_slot = jnp.arange(slots, dtype=jnp.int32)[None, :] < live[:, None]
-    zero_value = jnp.zeros((), grid_profiles.dtype)
-    outgoing = jnp.where(live_slot[:, :, None], grid_profiles[rows], zero_value)
-
-    zenith = angle_index.astype(jnp.float32) * (max_zenith / (NANG - 1))
-    slant_path = (1.0 / jnp.cos(zenith) - 1.0)[None, :]
-    jac = jnp.pad(jacobian.transpose(0, 2, 1), ((0, 0), (0, spare), (0, 0)))
-    jac = jac.reshape(3 * PADDED, DEPTH)
-    padded = jnp.pad(observed, ((0, spare), (0, 0)))
-    rates = jnp.broadcast_to(
-        jnp.pad(kappa, ((0, 0), (0, spare)))[:, :, None], (2, PADDED, XTRACK)
-    )
-    own_factor = jnp.pad(
-        factor.reshape(own_chan, MEMBERS, own_chan), ((0, spare), (0, 0), (0, spare))
-    )
     half_depth = MEMBERS * PADDED // 2
-    own_factor = own_factor.reshape(PADDED, 2, half_depth).transpose(1, 0, 2)
-
     vmem = pl.BlockSpec(memory_space=pltpu.VMEM)
     dma = pltpu.SemaphoreType.DMA
-    return pl.pallas_call(
+    weighted = pl.pallas_call(
         functools.partial(kernel, own_chan),
-        out_shape=jax.ShapeDtypeStruct((own_chan, pixel_count), jnp.float32),
-        in_specs=[vmem] * 6,
+        out_shape=jax.ShapeDtypeStruct((own_chan, pixel_count), jnp.bfloat16),
+        in_specs=[vmem, vmem, pl.BlockSpec(memory_space=pltpu.SMEM)] + [vmem] * 5,
         out_specs=vmem,
         scratch_shapes=[
+            pltpu.VMEM((2, XTRACK, DEPTH), jnp.bfloat16),
+            pltpu.VMEM((2, PADDED, half_depth), jnp.bfloat16),
+            pltpu.VMEM((3 * PADDED, DEPTH), jnp.bfloat16),
+            pltpu.VMEM((4, ROWS, XTRACK), jnp.float32),
             pltpu.VMEM((LINES, XTRACK, DEPTH), jnp.bfloat16),
             pltpu.VMEM((2, MEMBERS, PADDED, half_depth), jnp.bfloat16),
-            pltpu.VMEM((LINES + 6, PADDED, XTRACK), jnp.float32),
-            pltpu.VMEM((LINES + 4, PADDED, XTRACK), jnp.float32),
-            pltpu.VMEM((LINES + 2, PADDED, XTRACK), jnp.float32),
+            pltpu.VMEM((LINES + 6, ROWS, XTRACK), jnp.float32),
+            pltpu.VMEM((LINES + 4, ROWS, XTRACK), jnp.float32),
+            pltpu.VMEM((LINES + 2, ROWS, XTRACK), jnp.float32),
             pltpu.VMEM((LINES, PADDED, XTRACK), jnp.bfloat16),
             pltpu.VMEM((2, MEMBERS, PADDED, XTRACK), jnp.bfloat16),
             pltpu.VMEM((2, MEMBERS, PADDED, XTRACK), jnp.bfloat16),
@@ -464,7 +501,17 @@
             dma((MEMBERS,)),
         ],
         compiler_params=pltpu.CompilerParams(collective_id=0, has_side_effects=True),
-    )(outgoing, own_factor, jac, padded, slant_path, rates)
+    )(
+        grid_profiles,
+        send_lists[0],
+        counts,
+        angle_index[None, :],
+        jacobian.transpose(0, 2, 1),
+        observed,
+        kappa,
+        factor,
+    )
+    return weighted.astype(jnp.float32)
 
 
 def solution(mesh):

time: 81.8 us -> 70.2 us (0.86)
  local copies, waits for them, and re-layouts: 8 us -> 0 us
  Pallas kernels: 69.7 us -> 67.7 us
  other arithmetic: 3.35 us -> 1.85 us
    unnamed x12 -> x0, local copies, waits for them, and re-layouts: 2.55 us -> none
    pallas_call x1, Pallas kernels: 69.7 us -> 67.7 us  [on_device(): pl.pallas_call(functools.partial(kernel, own_chan), out_shape=jax.ShapeDt...]
    convert_element_type x0 -> x1, other arithmetic: none -> 1.85 us  [on_device(): return weighted.astype(jnp.float32)]
    pad x4 -> x0, local copies, waits for them, and re-layouts: 1.45 us -> none  [the longest x1 0.77 us: on_device(): padded = jnp.pad(observed, ((0, spare), (0, 0)))]
    unnamed x1 -> x0, other arithmetic: 1.32 us -> none
    broadcast_in_dim x1 -> x0, other arithmetic: 1.2 us -> none  [on_device(): slant_path = (1.0 / jnp.cos(zenith) - 1.0)[None, :]]
    reshape x3 -> x0, local copies, waits for them, and re-layouts: 1.19 us -> none  [the longest x2 0.94 us: on_device(): own_factor = own_factor.reshape(PADDED, 2, half_depth).transpose(1, 0, 2)]
    gather x1 -> x0, local copies, waits for them, and re-layouts: 1.15 us -> none  [on_device(): outgoing = jnp.where(live_slot[:, :, None], grid_profiles[rows], zero_value)]
where the time goes in v3:
time: 70.2 us; the launch traced here: 69.6 us
  Pallas kernels  67.7 us (96%)
  other arithmetic  1.85 us (3%)
    pallas_call x1, Pallas kernels, on_device(): pl.pallas_call(functools.partial(kernel, own_chan), out_shape=jax.ShapeDt...  67.7 us
    convert_element_type x1, other arithmetic, on_device(): return weighted.astype(jnp.float32)  1.85 us

profile of v3, /device:TPU:1, one launch (start us, length us, event | category | flops | bytes accessed | tf_op | source)
XLA Modules:
  0.0 69.6 jit_solution(15626635979160813153)
XLA Ops:
  0.0 67.7 %shard_map.82 = bf16[38,4096]{1,0:T(8,128)(2,1)} custom-call(bf16[1024,256]{1,0:T(8,128)(2,1)} %grid.1, s32[32,128]{1,0:T(8,128)} %bitcast.4, s32[1,32]{1,0:T(1,128)} %counts.1, s32[1,128]{1,0:T(1,128)} %bitcast.5, bf16[3,38,256]{2,1,0:T(8,128)(2,1)} %bitcast.3, bf16[38,4096]{1,0:T(8,128)(2,1)} %observed.1, f32[2,38]{1,0:T(2,128)} %kappa.1, ...), custom_call_target="tpu_custom_call" | custom-call | tf_op jit(solution)/shard_map/pallas_call | solution.py:472
  67.7 1.9 %convert_element_type.3 = f32[38,4096]{1,0:T(8,128)} convert(bf16[38,4096]{1,0:T(8,128)(2,1)} %shard_map.82) | non-fusion elementwise | flops 155648 | bytes 933888 | tf_op jit(solution)/shard_map/convert_element_type | solution.py:514

commit v4 on v3

--- a/solution.py
+++ b/solution.py
@@ -26,13 +26,18 @@
 
 def kernel(
     own_chan,
-    grid,
+    grid_in,
     lists,
     counts,
     angle,
+    jac_held,
+    observed_in,
+    kappa,
+    factor_held,
+    result,
+    grid,
     jac_in,
     observed,
-    kappa,
     factor_in,
     out,
     outgoing,
@@ -59,6 +64,8 @@
     there_recv,
     back_send,
     back_recv,
+    load_sem,
+    store_sem,
 ):
     swath = lax.axis_index("swath")
     chan = lax.axis_index("chan")
@@ -88,6 +95,16 @@
         def _():
             pl.semaphore_signal(barrier, inc=1, device_id={"swath": other}, device_id_type=MESH)
 
+    loads = [
+        pltpu.make_async_copy(held, block, load_sem.at[i])
+        for i, (held, block) in enumerate(
+            ((grid_in, grid), (factor_held, factor_in), (jac_held, jac_in), (observed_in, observed))
+        )
+    ]
+    for load in loads:
+        load.start()
+
+    loads[0].wait()
     grid_rows = grid.shape[0]
     slot = lax.broadcasted_iota(jnp.int32, (1, XTRACK), 1)
     grid_row = lax.broadcasted_iota(jnp.int32, (grid_rows, XTRACK), 0)
@@ -105,6 +122,7 @@
     target = jnp.where(place - owner * PADDED < own_chan, place - owner * (PADDED - own_chan), -1)
     source_row = lax.broadcasted_iota(jnp.int32, (channels, MEMBERS * PADDED), 0)
     spread = jnp.where(source_row == target, 1.0, 0.0).astype(jnp.bfloat16)
+    loads[1].wait()
     spaced = jnp.dot(factor_in[...], spread, preferred_element_type=jnp.float32)
     spaced = spaced.astype(jnp.bfloat16)
     half_depth = MEMBERS * PADDED // 2
@@ -112,6 +130,8 @@
     for k in range(2):
         own_factor[k, pl.ds(0, own_chan)] = spaced[:, k * half_depth : (k + 1) * half_depth]
 
+    loads[2].wait()
+    loads[3].wait()
     jac[...] = jnp.zeros(jac.shape, jnp.bfloat16)
     for m in range(3):
         jac[pl.ds(m * PADDED, own_chan)] = jac_in[m]
@@ -327,9 +347,6 @@
         edges.append(copy)
         sent.append(copy)
 
-    for copy in edges:
-        copy.wait_recv()
-
     def clear(block, width):
         @pl.when(swath == 0)
         def _():
@@ -351,22 +368,15 @@
             + (weight[2] * left + weight[3] * right)
         )
 
-    def sweep(source, target, count, step):
+    def sweep(source, target, start, count, step):
         @pl.loop(0, count // step)
         def _(turn):
             for i in range(step):
-                target[step * turn + i] = diffuse(source, step * turn + i + 1)
-
-        for at in range(count - count % step, count):
+                at = start + step * turn + i
+                target[at] = diffuse(source, at + 1)
+
+        for at in range(start + count - count % step, start + count):
             target[at] = diffuse(source, at + 1)
-
-    clear(field, 3)
-
-    sweep(field, field_1, LINES + 4, 6)
-    clear(field_1, 2)
-
-    sweep(field_1, field_2, LINES + 2, 6)
-    clear(field_2, 1)
 
     def there(who, into):
         return pltpu.make_async_remote_copy(
@@ -378,18 +388,45 @@
             device_id_type=MESH,
         )
 
-    def smooth_pair(i):
-        who = lax.rem(chan + 1 + i, MEMBERS)
+    def smooth_pair(who):
         for j in range(2):
             value = diffuse(field_2, 2 * who + j + 1).astype(jnp.bfloat16)
             smoothed[2 * who + j, pl.ds(0, ROWS)] = value
 
-    smooth_pair(0)
-
-    @pl.loop(1, MEMBERS)
+    def send_pair(who):
+        @pl.when(who != chan)
+        def _():
+            there(who, chan).start()
+
+    inner = MEMBERS - 4
+
+    def inner_member(i):
+        return 2 + lax.rem(chan + i, inner)
+
+    sweep(field, field_1, SWEEPS, LINES - 2, 6)
+    sweep(field_1, field_2, SWEEPS, LINES - 4, 7)
+    smooth_pair(inner_member(0))
+
+    @pl.loop(1, inner)
     def _(i):
-        smooth_pair(i)
-        there(lax.rem(chan + i, MEMBERS), chan).start()
+        smooth_pair(inner_member(i))
+        send_pair(inner_member(i - 1))
+
+    for copy in edges:
+        copy.wait_recv()
+    clear(field, 3)
+    for start in (0, LINES + 1):
+        sweep(field, field_1, start, 3, 3)
+    clear(field_1, 2)
+    for start in (0, LINES - 1):
+        sweep(field_1, field_2, start, 3, 3)
+    clear(field_2, 1)
+    send_pair(inner_member(inner - 1))
+    outer = (0, MEMBERS - 1, 1, MEMBERS - 2)
+    for who in outer:
+        smooth_pair(who)
+    for who in outer:
+        send_pair(who)
 
     for j in range(2):
         every[j, chan] = smoothed[2 * chan + j]
@@ -414,9 +451,6 @@
             part = block[:, j * XTRACK : (j + 1) * XTRACK].astype(jnp.bfloat16)
             product[j, pl.ds(group * GROUP, GROUP)] = part.reshape(GROUP, PADDED, XTRACK)
 
-    for group in range(MEMBERS // GROUP):
-        weigh(group)
-
     def back(who, into):
         return pltpu.make_async_remote_copy(
             src_ref=product.at[:, who],
@@ -427,9 +461,24 @@
             device_id_type=MESH,
         )
 
-    @pl.loop(1, MEMBERS)
-    def _(i):
-        back(lax.rem(chan + i, MEMBERS), chan).start()
+    groups = MEMBERS // GROUP
+
+    def group_at(i):
+        return lax.rem(chan // GROUP + 1 + i, groups)
+
+    def send_group(group):
+        for i in range(GROUP):
+            who = group * GROUP + lax.rem(chan + i, GROUP)
+
+            @pl.when(who != chan)
+            def _():
+                back(who, chan).start()
+
+    for i in range(groups):
+        weigh(group_at(i))
+        if i > 0:
+            send_group(group_at(i - 1))
+    send_group(group_at(groups - 1))
 
     for j in range(2):
         arrived[2 * chan + j] = product[j, chan]
@@ -440,6 +489,12 @@
             columns = pl.ds(pl.multiple_of(at * XTRACK, XTRACK), XTRACK)
             out[:, columns] = arrived[at, pl.ds(0, own_chan)]
 
+    def store(who):
+        columns = pl.ds(pl.multiple_of(2 * who * XTRACK, 2 * XTRACK), 2 * XTRACK)
+        return pltpu.make_async_copy(
+            out.at[:, columns], result.at[:, columns], store_sem.at[who]
+        )
+
     settle(chan)
 
     @pl.loop(1, MEMBERS)
@@ -447,6 +502,7 @@
         who = lax.rem(chan + i, MEMBERS)
         back(who, who).wait_recv()
         settle(who)
+        store(lax.rem(chan + i - 1, MEMBERS)).start()
 
     for copy in sent:
         copy.wait_send()
@@ -455,6 +511,8 @@
         @pl.when(partners[k] != swath)
         def _():
             slot_copy(k).wait_send()
+
+    store(lax.rem(chan + MEMBERS - 1, MEMBERS)).start()
 
     @pl.loop(1, MEMBERS)
     def _(i):
@@ -462,19 +520,29 @@
         there(who, chan).wait_send()
         back(who, chan).wait_send()
 
+    @pl.loop(0, MEMBERS)
+    def _(who):
+        store(who).wait()
+
 
 def on_device(grid_profiles, send_lists, counts, angle_index, jacobian, observed, kappa, factor):
     own_chan = observed.shape[0]
     pixel_count = observed.shape[1]
     half_depth = MEMBERS * PADDED // 2
     vmem = pl.BlockSpec(memory_space=pltpu.VMEM)
+    held = pl.BlockSpec(memory_space=pl.ANY)
     dma = pltpu.SemaphoreType.DMA
     weighted = pl.pallas_call(
         functools.partial(kernel, own_chan),
         out_shape=jax.ShapeDtypeStruct((own_chan, pixel_count), jnp.bfloat16),
-        in_specs=[vmem, vmem, pl.BlockSpec(memory_space=pltpu.SMEM)] + [vmem] * 5,
-        out_specs=vmem,
+        in_specs=[held, vmem, pl.BlockSpec(memory_space=pltpu.SMEM), vmem, held, held, vmem, held],
+        out_specs=held,
         scratch_shapes=[
+            pltpu.VMEM(grid_profiles.shape, jnp.bfloat16),
+            pltpu.VMEM((3, own_chan, DEPTH), jnp.bfloat16),
+            pltpu.VMEM(observed.shape, jnp.bfloat16),
+            pltpu.VMEM(factor.shape, jnp.bfloat16),
+            pltpu.VMEM(observed.shape, jnp.bfloat16),
             pltpu.VMEM((2, XTRACK, DEPTH), jnp.bfloat16),
             pltpu.VMEM((2, PADDED, half_depth), jnp.bfloat16),
             pltpu.VMEM((3 * PADDED, DEPTH), jnp.bfloat16),
@@ -499,6 +567,8 @@
             dma((MEMBERS,)),
             dma((MEMBERS,)),
             dma((MEMBERS,)),
+            dma((4,)),
+            dma((MEMBERS,)),
         ],
         compiler_params=pltpu.CompilerParams(collective_id=0, has_side_effects=True),
     )(

time: 70.2 us -> 65.8 us (0.937)
  Pallas kernels: 67.7 us -> 63.3 us
    pallas_call x1, Pallas kernels: 67.7 us -> 63.3 us  [on_device(): pl.pallas_call(functools.partial(kernel, own_chan), out_shape=jax.ShapeDt...]
where the time goes in v4:
time: 65.8 us; the launch traced here: 65.2 us
  Pallas kernels  63.3 us (96%)
  other arithmetic  1.85 us (3%)
    pallas_call x1, Pallas kernels, on_device(): pl.pallas_call(functools.partial(kernel, own_chan), out_shape=jax.ShapeDt...  63.3 us
    convert_element_type x1, other arithmetic, on_device(): return weighted.astype(jnp.float32)  1.85 us

profile of v4, /device:TPU:1, one launch (start us, length us, event | category | flops | bytes accessed | tf_op | source)
XLA Modules:
  0.0 65.2 jit_solution(5414463988698603711)
XLA Ops:
  0.0 63.3 %shard_map.82 = bf16[38,4096]{1,0:T(8,128)(2,1)} custom-call(bf16[1024,256]{1,0:T(8,128)(2,1)} %grid_in.1, s32[32,128]{1,0:T(8,128)} %bitcast.4, s32[1,32]{1,0:T(1,128)} %counts.1, s32[1,128]{1,0:T(1,128)} %bitcast.5, bf16[3,38,256]{2,1,0:T(8,128)(2,1)} %bitcast.3, bf16[38,4096]{1,0:T(8,128)(2,1)} %observed_in.1, f32[2,38]{1,0:T(2,128)} %kappa.1, ...), custom_call_target="tpu_custom_call" | custom-call | tf_op jit(solution)/shard_map/pallas_call | solution.py:535
  63.3 1.9 %convert_element_type.3 = f32[38,4096]{1,0:T(8,128)} convert(bf16[38,4096]{1,0:T(8,128)(2,1)} %shard_map.82) | non-fusion elementwise | flops 155648 | bytes 933888 | tf_op jit(solution)/shard_map/convert_element_type | solution.py:584

commit v5 on v4

--- a/solution.py
+++ b/solution.py
@@ -19,6 +19,7 @@
 PADDED = 48
 ROWS = 40
 GROUP = 4
+PARTS = 2
 MESH = pl.DeviceIdType.MESH
 
 max_zenith = math.pi / 3.0
@@ -141,46 +142,46 @@
     distinct = sum(jnp.where(other != swath, 1, 0) for other in partners)
     pl.semaphore_wait(barrier, MEMBERS + 1 + distinct)
 
-    def slot_copy(k):
+    part_rows = XTRACK // PARTS
+
+    def part_of(block, part):
+        return block.at[pl.ds(part * part_rows, part_rows)]
+
+    def slot_copy(k, part, half):
         return pltpu.make_async_remote_copy(
-            src_ref=outgoing.at[k],
-            dst_ref=profiles.at[swath],
-            send_sem=slot_send.at[k],
-            recv_sem=slot_recv.at[k],
+            src_ref=part_of(outgoing.at[k], part),
+            dst_ref=part_of(profiles.at[swath], part),
+            send_sem=slot_send.at[k * PARTS + part],
+            recv_sem=slot_recv.at[half * PARTS + part],
             device_id={"swath": partners[k]},
             device_id_type=MESH,
         )
 
-    def slot_kept(k):
-        return pltpu.make_async_copy(outgoing.at[k], profiles.at[swath], slot_local.at[k])
-
-    def slot_sent(k):
-        half = swath // MEMBERS
-        return pltpu.make_async_remote_copy(
-            src_ref=outgoing.at[k],
-            dst_ref=profiles.at[swath],
-            send_sem=slot_send.at[k],
-            recv_sem=slot_recv.at[half],
-            device_id={"swath": partners[k]},
-            device_id_type=MESH,
-        )
-
-    for k in range(2):
-
-        @pl.when(partners[k] != swath)
-        def _():
-            slot_sent(k).start()
-
-        @pl.when(partners[k] == swath)
-        def _():
-            slot_kept(k).start()
-
-    def profile_piece(route, who):
-        return profiles.at[line_of(route, who)]
-
-    def profile_half(route, who, half):
-        rows = XTRACK // 2
-        return profiles.at[line_of(route, who), pl.ds(half * rows, rows)]
+    def slot_kept(k, part):
+        return pltpu.make_async_copy(
+            part_of(outgoing.at[k], part),
+            part_of(profiles.at[swath], part),
+            slot_local.at[k * PARTS + part],
+        )
+
+    for part in range(PARTS):
+        for k in range(2):
+
+            @pl.when(partners[k] != swath)
+            def _():
+                slot_copy(k, part, swath // MEMBERS).start()
+
+            @pl.when(partners[k] == swath)
+            def _():
+                slot_kept(k, part).start()
+
+    def profile_piece(part, route, who):
+        return part_of(profiles.at[line_of(route, who)], part)
+
+    def profile_half(part, route, who, half):
+        rows = part_rows // 2
+        start = part * part_rows + half * rows
+        return profiles.at[line_of(route, who), pl.ds(start, rows)]
 
     def factor_piece(route, who):
         return factor.at[route, who]
@@ -197,7 +198,7 @@
             self.copies = {}
 
         def send(self, key, number, source, target, to):
-            at = (self.kind * 2 + self.route) * 20 + number
+            at = self.kind * 20 + number
             copy = pltpu.make_async_remote_copy(
                 src_ref=source,
                 dst_ref=target,
@@ -223,19 +224,18 @@
             for way in range(2):
                 to = member(self.route, 1 - 2 * way, 0)
                 self.send(("a", way), way, target if source is None else source, target, to)
+            to = member(self.route, 2, 0)
+            self.send(("c", 0), 2, target if source is None else source, target, to)
             self.whole(0, source)
 
         def relay(self):
             for way in range(2):
                 self.copies["a", way].wait_recv()
                 came = 2 * way - 1
-                part = self.half(self.route, member(self.route, came, 0), way)
-                self.send(("c", way), 2 + way, part, part, member(self.route, -came, 0))
                 self.whole(came)
 
         def across(self):
-            for way in range(2):
-                self.copies["c", way].wait_recv()
+            self.copies["c", 0].wait_recv()
             self.whole(2)
 
         def finish(self):
@@ -252,8 +252,17 @@
                 for way in range(2):
                     self.copies["d", offset, way].wait_recv()
 
-    profile_rings = [Ring(0, k, profile_piece, profile_half) for k in range(2)]
-    factor_rings = [Ring(1, k, factor_piece, factor_half) for k in range(2)]
+    factor_rings = [Ring(k, k, factor_piece, factor_half) for k in range(2)]
+    profile_rings = [
+        Ring(
+            2 + part * 2 + k,
+            k,
+            functools.partial(profile_piece, part),
+            functools.partial(profile_half, part),
+        )
+        for part in range(PARTS)
+        for k in range(2)
+    ]
 
     for k, ring in enumerate(factor_rings):
         ring.open(own_factor.at[k])
@@ -263,25 +272,26 @@
         ring.relay()
     for ring in factor_rings:
         ring.across()
-    for k, ring in enumerate(profile_rings):
+    for i, ring in enumerate(profile_rings):
+        part, k = i // 2, i % 2
 
         @pl.when(partners[k] != swath)
         def _():
-            slot_copy(k).wait_recv()
+            slot_copy(k, part, k).wait_recv()
 
         @pl.when(partners[k] == swath)
         def _():
-            slot_kept(k).wait()
+            slot_kept(k, part).wait()
 
         ring.open()
-    for ring in factor_rings:
-        ring.finish()
     for ring in profile_rings:
         ring.relay()
     for ring in profile_rings:
         ring.across()
     for ring in profile_rings:
         ring.finish()
+    for ring in factor_rings:
+        ring.finish()
     zenith = angle[...].astype(jnp.float32) * (max_zenith / (NANG - 1))
     path = 1.0 / jnp.cos(zenith) - 1.0
     path_2 = path * path
@@ -307,8 +317,6 @@
             for first in offsets:
                 depart(route, first, i - 1)
 
-    for ring in factor_rings:
-        ring.close()
     for ring in profile_rings:
         ring.close()
     for route in range(2):
@@ -436,6 +444,9 @@
         who = lax.rem(chan + i, MEMBERS)
         there(who, who).wait_recv()
 
+    for ring in factor_rings:
+        ring.close()
+
     pieces = [every[j].reshape(MEMBERS * PADDED, XTRACK) for j in range(2)]
     wide = jnp.concatenate(pieces, axis=1)
 
@@ -510,7 +521,8 @@
 
         @pl.when(partners[k] != swath)
         def _():
-            slot_copy(k).wait_send()
+            for part in range(PARTS):
+                slot_copy(k, part, k).wait_send()
 
     store(lax.rem(chan + MEMBERS - 1, MEMBERS)).start()
 
@@ -556,11 +568,11 @@
             pltpu.VMEM((2, MEMBERS, PADDED, XTRACK), jnp.bfloat16),
             pltpu.VMEM((2, MEMBERS, PADDED, XTRACK), jnp.bfloat16),
             pltpu.VMEM((LINES, PADDED, XTRACK), jnp.bfloat16),
-            dma((2,)),
-            dma((2,)),
-            dma((2,)),
-            dma((80,)),
-            dma((80,)),
+            dma((2 * PARTS,)),
+            dma((2 * PARTS,)),
+            dma((2 * PARTS,)),
+            dma((40 + 40 * PARTS,)),
+            dma((40 + 40 * PARTS,)),
             dma((2,)),
             dma((2,)),
             dma((MEMBERS,)),

time: 65.8 us -> 63.5 us (0.965)
  the two profiles are of different devices: /device:TPU:1 before, /device:TPU:32 now
where the time goes in v5:
time: 63.5 us; the launch traced here: 63.3 us
  Pallas kernels  61.4 us (97%)
  other arithmetic  1.85 us (3%)
    pallas_call x1, Pallas kernels, on_device(): pl.pallas_call(functools.partial(kernel, own_chan), out_shape=jax.ShapeDt...  61.4 us
    convert_element_type x1, other arithmetic, on_device(): return weighted.astype(jnp.float32)  1.85 us

profile of v5, /device:TPU:32, one launch (start us, length us, event | category | flops | bytes accessed | tf_op | source)
XLA Modules:
  0.0 63.3 jit_solution(7424076363202158374)
XLA Ops:
  0.0 61.4 %shard_map.82 = bf16[38,4096]{1,0:T(8,128)(2,1)} custom-call(bf16[1024,256]{1,0:T(8,128)(2,1)} %grid_in.1, s32[32,128]{1,0:T(8,128)} %bitcast.4, s32[1,32]{1,0:T(1,128)} %counts.1, s32[1,128]{1,0:T(1,128)} %bitcast.5, bf16[3,38,256]{2,1,0:T(8,128)(2,1)} %bitcast.3, bf16[38,4096]{1,0:T(8,128)(2,1)} %observed_in.1, f32[2,38]{1,0:T(2,128)} %kappa.1, ...), custom_call_target="tpu_custom_call" | custom-call | tf_op jit(solution)/shard_map/pallas_call | solution.py:547
  61.4 1.9 %convert_element_type.3 = f32[38,4096]{1,0:T(8,128)} convert(bf16[38,4096]{1,0:T(8,128)(2,1)} %shard_map.82) | non-fusion elementwise | flops 155648 | bytes 933888 | tf_op jit(solution)/shard_map/convert_element_type | solution.py:596

commit v6 on v5

--- a/solution.py
+++ b/solution.py
@@ -118,10 +118,10 @@
         ).astype(jnp.bfloat16)
 
     channels = MEMBERS * own_chan
-    place = lax.broadcasted_iota(jnp.int32, (1, MEMBERS * PADDED), 1)
-    owner = sum(jnp.where(place >= m * PADDED, 1, 0) for m in range(1, MEMBERS))
-    target = jnp.where(place - owner * PADDED < own_chan, place - owner * (PADDED - own_chan), -1)
-    source_row = lax.broadcasted_iota(jnp.int32, (channels, MEMBERS * PADDED), 0)
+    place = lax.broadcasted_iota(jnp.int32, (1, MEMBERS * ROWS), 1)
+    owner = sum(jnp.where(place >= m * ROWS, 1, 0) for m in range(1, MEMBERS))
+    target = jnp.where(place - owner * ROWS < own_chan, place - owner * (ROWS - own_chan), -1)
+    source_row = lax.broadcasted_iota(jnp.int32, (channels, MEMBERS * ROWS), 0)
     spread = jnp.where(source_row == target, 1.0, 0.0).astype(jnp.bfloat16)
     loads[1].wait()
     spaced = jnp.dot(factor_in[...], spread, preferred_element_type=jnp.float32)
@@ -129,15 +129,14 @@
     half_depth = MEMBERS * PADDED // 2
     own_factor[...] = jnp.zeros(own_factor.shape, jnp.bfloat16)
     for k in range(2):
-        own_factor[k, pl.ds(0, own_chan)] = spaced[:, k * half_depth : (k + 1) * half_depth]
+        first = k * (MEMBERS * ROWS - half_depth)
+        own_factor[k, pl.ds(0, own_chan)] = spaced[:, first : first + half_depth]
 
     loads[2].wait()
     loads[3].wait()
     jac[...] = jnp.zeros(jac.shape, jnp.bfloat16)
     for m in range(3):
         jac[pl.ds(m * PADDED, own_chan)] = jac_in[m]
-
-    smoothed[...] = jnp.zeros(smoothed.shape, jnp.bfloat16)
 
     distinct = sum(jnp.where(other != swath, 1, 0) for other in partners)
     pl.semaphore_wait(barrier, MEMBERS + 1 + distinct)
@@ -388,8 +387,8 @@
 
     def there(who, into):
         return pltpu.make_async_remote_copy(
-            src_ref=smoothed.at[pl.ds(2 * who, 2)],
-            dst_ref=every.at[:, into],
+            src_ref=smoothed.at[who],
+            dst_ref=every.at[into],
             send_sem=there_send.at[who],
             recv_sem=there_recv.at[into],
             device_id={"chan": who},
@@ -397,9 +396,8 @@
         )
 
     def smooth_pair(who):
-        for j in range(2):
-            value = diffuse(field_2, 2 * who + j + 1).astype(jnp.bfloat16)
-            smoothed[2 * who + j, pl.ds(0, ROWS)] = value
+        pair = [diffuse(field_2, 2 * who + j + 1) for j in range(2)]
+        smoothed[who] = jnp.concatenate(pair, axis=0).astype(jnp.bfloat16)
 
     def send_pair(who):
         @pl.when(who != chan)
@@ -436,8 +434,7 @@
     for who in outer:
         send_pair(who)
 
-    for j in range(2):
-        every[j, chan] = smoothed[2 * chan + j]
+    every[chan] = smoothed[chan]
 
     @pl.loop(1, MEMBERS)
     def _(i):
@@ -447,8 +444,11 @@
     for ring in factor_rings:
         ring.close()
 
-    pieces = [every[j].reshape(MEMBERS * PADDED, XTRACK) for j in range(2)]
-    wide = jnp.concatenate(pieces, axis=1)
+    pairs = [every[m].astype(jnp.float32) for m in range(MEMBERS)]
+    wide = jnp.concatenate(
+        [jnp.concatenate([pair[:ROWS], pair[ROWS:]], axis=1) for pair in pairs], axis=0
+    ).astype(jnp.bfloat16)
+    overlap = 2 * half_depth - MEMBERS * ROWS
 
     def weigh(group):
         rows = [
@@ -457,15 +457,19 @@
         ]
         block = jnp.dot(
             rows[0], wide[:half_depth], preferred_element_type=jnp.float32
-        ) + jnp.dot(rows[1], wide[half_depth:], preferred_element_type=jnp.float32)
-        for j in range(2):
-            part = block[:, j * XTRACK : (j + 1) * XTRACK].astype(jnp.bfloat16)
-            product[j, pl.ds(group * GROUP, GROUP)] = part.reshape(GROUP, PADDED, XTRACK)
+        ) + jnp.dot(
+            rows[1][:, overlap:], wide[half_depth:], preferred_element_type=jnp.float32
+        )
+        for i in range(GROUP):
+            part = block[i * PADDED : i * PADDED + ROWS]
+            product[group * GROUP + i] = jnp.concatenate(
+                [part[:, :XTRACK], part[:, XTRACK:]], axis=0
+            ).astype(jnp.bfloat16)
 
     def back(who, into):
         return pltpu.make_async_remote_copy(
-            src_ref=product.at[:, who],
-            dst_ref=arrived.at[pl.ds(2 * into, 2)],
+            src_ref=product.at[who],
+            dst_ref=arrived.at[into],
             send_sem=back_send.at[who],
             recv_sem=back_recv.at[into],
             device_id={"chan": who},
@@ -491,14 +495,13 @@
             send_group(group_at(i - 1))
     send_group(group_at(groups - 1))
 
-    for j in range(2):
-        arrived[2 * chan + j] = product[j, chan]
+    arrived[chan] = product[chan]
 
     def settle(who):
+        pair = arrived[who].astype(jnp.float32)
         for j in range(2):
-            at = 2 * who + j
-            columns = pl.ds(pl.multiple_of(at * XTRACK, XTRACK), XTRACK)
-            out[:, columns] = arrived[at, pl.ds(0, own_chan)]
+            columns = pl.ds(pl.multiple_of((2 * who + j) * XTRACK, XTRACK), XTRACK)
+            out[:, columns] = pair[j * ROWS : j * ROWS + own_chan].astype(jnp.bfloat16)
 
     def store(who):
         columns = pl.ds(pl.multiple_of(2 * who * XTRACK, 2 * XTRACK), 2 * XTRACK)
@@ -564,10 +567,10 @@
             pltpu.VMEM((LINES + 6, ROWS, XTRACK), jnp.float32),
             pltpu.VMEM((LINES + 4, ROWS, XTRACK), jnp.float32),
             pltpu.VMEM((LINES + 2, ROWS, XTRACK), jnp.float32),
-            pltpu.VMEM((LINES, PADDED, XTRACK), jnp.bfloat16),
-            pltpu.VMEM((2, MEMBERS, PADDED, XTRACK), jnp.bfloat16),
-            pltpu.VMEM((2, MEMBERS, PADDED, XTRACK), jnp.bfloat16),
-            pltpu.VMEM((LINES, PADDED, XTRACK), jnp.bfloat16),
+            pltpu.VMEM((MEMBERS, 2 * ROWS, XTRACK), jnp.bfloat16),
+            pltpu.VMEM((MEMBERS, 2 * ROWS, XTRACK), jnp.bfloat16),
+            pltpu.VMEM((MEMBERS, 2 * ROWS, XTRACK), jnp.bfloat16),
+            pltpu.VMEM((MEMBERS, 2 * ROWS, XTRACK), jnp.bfloat16),
             dma((2 * PARTS,)),
             dma((2 * PARTS,)),
             dma((2 * PARTS,)),

time: 63.5 us -> 62.3 us (0.981)
  the two profiles are of different devices: /device:TPU:32 before, /device:TPU:4 now
where the time goes in v6:
time: 62.3 us; the launch traced here: 62.1 us
  Pallas kernels  60.2 us (97%)
  other arithmetic  1.85 us (3%)
    pallas_call x1, Pallas kernels, on_device(): pl.pallas_call(functools.partial(kernel, own_chan), out_shape=jax.ShapeDt...  60.2 us
    convert_element_type x1, other arithmetic, on_device(): return weighted.astype(jnp.float32)  1.85 us

profile of v6, /device:TPU:4, one launch (start us, length us, event | category | flops | bytes accessed | tf_op | source)
XLA Modules:
  0.0 62.1 jit_solution(605431565523145464)
XLA Ops:
  0.0 60.2 %shard_map.82 = bf16[38,4096]{1,0:T(8,128)(2,1)} custom-call(bf16[1024,256]{1,0:T(8,128)(2,1)} %grid_in.1, s32[32,128]{1,0:T(8,128)} %bitcast.4, s32[1,32]{1,0:T(1,128)} %counts.1, s32[1,128]{1,0:T(1,128)} %bitcast.5, bf16[3,38,256]{2,1,0:T(8,128)(2,1)} %bitcast.3, bf16[38,4096]{1,0:T(8,128)(2,1)} %observed_in.1, f32[2,38]{1,0:T(2,128)} %kappa.1, ...), custom_call_target="tpu_custom_call" | custom-call | tf_op jit(solution)/shard_map/pallas_call | solution.py:550
  60.2 1.9 %convert_element_type.3 = f32[38,4096]{1,0:T(8,128)} convert(bf16[38,4096]{1,0:T(8,128)(2,1)} %shard_map.82) | non-fusion elementwise | flops 155648 | bytes 933888 | tf_op jit(solution)/shard_map/convert_element_type | solution.py:599
